TPU v7x, 512 devices: a whole 4x8x8 slice. The times are simulated.
512 devices in a mesh: wide: 64 (over y, z), narrow: 8 (over x, core).
Axes of the slice: x: 4, y: 8, z: 8, core: 2. Of those that a mesh axis runs over, the one named last changes fastest.
Arguments:
- haze_bin_mass: float32 [4096, 256, 128], P('wide', 'narrow'), may hold values from 0.05 to 2
- wind_speed: float32 [4096, 256], P('wide', 'narrow'), may hold values from 0.1 to 0.9
- vapour: float32 [4096, 256], P('wide', 'narrow'), may hold values from 0.2 to 2
- uptake_rates: float32 [128], replicated, may hold values from 0.05 to 1
- coag_left: float32 [128, 8], replicated, may hold values from -0.5 to 0.5
- coag_right: float32 [128, 8], replicated, may hold values from -0.5 to 0.5
- coag_gain: float32 [8, 128], replicated, may hold values from -2 to 2
- coag_loss: float32 [8, 128], replicated, may hold values from -2 to 2
- targets: int32 [4096, 1], replicated, may hold values from 0 to 63; in each aligned block of 64 rows (0 to 63, 64 to 127, ...) at most 2 rows name the same one
- upwind_blocks: int32 [4096], replicated, may hold values from 0 to 4095, as said below
Outputs:
- haze_output_slots: float32 [8192, 256, 128], P('wide', 'narrow')
- vapour_out: float32 [4096, 256], P('wide', 'narrow')
Inputs may be any that keep to these rules, and one draw needn't show every extreme that they name: `targets`: among the 64 rows of one aligned block of rows no owner appears more than 2 times, and some owner appears exactly 2 times. upwind_blocks[b] // 64 equals b // 64, or the index one above or one below it, counted cyclically over the 64 owners.
All inputs are finite; a program needn't handle non-finite values.
Results may differ from a plain program's by a relative error of at most 0.000073.
Values sent between devices are 32-bit elements; how exact they have to be, the bound alone decides.
No kernel may reach another device: no remote copies, remote signals or barrier semaphores. Data moves between devices by JAX's collectives and lax.ppermute only.
A program may use at most 64 MiB of HBM per device.

v0:
```python
import jax
import jax.numpy as jnp
from jax import lax
from jax.sharding import PartitionSpec as P

PRECISE = lax.Precision.HIGHEST
STEP_DT = 0.25


def passed_along(block, axis, distance):
    devices = range(lax.axis_size(axis))
    route = [((i - distance) % len(devices), i) for i in devices]
    return lax.ppermute(block, axis, route)


def extended(block, sides, width):
    for axis, dim in sides:
        count = lax.axis_size(axis)
        forward = [(i, i + 1) for i in range(count - 1)]
        forward.append((count - 1, 0))
        backward = [(target, source) for source, target in forward]
        low = lax.ppermute(
            lax.slice_in_dim(block, block.shape[dim] - width, None, axis=dim), axis, forward
        )
        high = lax.ppermute(lax.slice_in_dim(block, 0, width, axis=dim), axis, backward)
        block = jnp.concatenate([low, block, high], axis=dim)
    return block


def microphysics(haze_bin_mass, vapour, uptake_rates, coag_left, coag_right, coag_gain, coag_loss):
    flat_rows = haze_bin_mass.reshape(-1, haze_bin_mass.shape[-1])
    left_proj = jnp.dot(flat_rows, coag_left, precision=PRECISE, preferred_element_type=jnp.float32)
    right_proj = jnp.dot(
        flat_rows, coag_right, precision=PRECISE, preferred_element_type=jnp.float32
    )
    coagulation_kernel_rate = jnp.dot(
        left_proj * right_proj, coag_gain, precision=PRECISE, preferred_element_type=jnp.float32
    )
    coagulation_kernel_rate = coagulation_kernel_rate - flat_rows * jnp.dot(
        left_proj, coag_loss, precision=PRECISE, preferred_element_type=jnp.float32
    )
    coagulation_kernel_rate = coagulation_kernel_rate.reshape(haze_bin_mass.shape)
    mean_take = jnp.mean(haze_bin_mass * uptake_rates, axis=-1)
    factor = 1.0 / (1.0 + vapour * mean_take)
    uptake = (vapour * factor)[..., None] * uptake_rates * haze_bin_mass
    grown_mass = haze_bin_mass + STEP_DT * coagulation_kernel_rate + uptake
    return (grown_mass, vapour * factor)


def advect(grown_mass, inflow, wind_speed):
    upwind_row = jnp.concatenate([inflow[:, None, :], grown_mass[:, :-1, :]], axis=1)
    return grown_mass - wind_speed[..., None] * (grown_mass - upwind_row)


def slot_tables(targets, wide_count, block_dev):
    owner_table = targets[:, 0]
    capacity = max(2, 2 * block_dev // wide_count)
    grouped = owner_table.reshape(wide_count, block_dev)
    same_target = grouped[:, :, None] == grouped[:, None, :]
    positions = jnp.arange(block_dev)
    earlier = positions[None, :] < positions[:, None]
    rank_within = jnp.sum(same_target & earlier[None], axis=2).reshape(-1)
    source = jnp.arange(owner_table.shape[0]) // block_dev
    return (owner_table, source * capacity + rank_within, capacity)


def local(
    haze_bin_mass,
    wind_speed,
    vapour,
    uptake_rates,
    coag_left,
    coag_right,
    coag_gain,
    coag_loss,
    targets,
    upwind_blocks,
):
    wide_count = lax.axis_size("wide")
    block_dev, cell_count, bin_count = haze_bin_mass.shape
    owner_index = lax.axis_index("wide")
    owner_table, local_slot_index, capacity = slot_tables(targets, wide_count, block_dev)
    slot_count = wide_count * capacity
    mine_owner = lax.dynamic_slice_in_dim(owner_table, owner_index * block_dev, block_dev)
    mine_slot = lax.dynamic_slice_in_dim(local_slot_index, owner_index * block_dev, block_dev)
    send_pos = mine_owner * capacity + mine_slot - owner_index * capacity
    positions = jnp.arange(block_dev, dtype=jnp.int32)
    slot_source = jnp.zeros((slot_count,), jnp.int32).at[send_pos].set(positions)
    slot_filled = jnp.zeros((slot_count,), jnp.float32).at[send_pos].set(1.0)
    top_row = lax.axis_index("narrow") == 0
    grown_mass, vapour_out = microphysics(
        haze_bin_mass, vapour, uptake_rates, coag_left, coag_right, coag_gain, coag_loss
    )
    rim_cells = passed_along(grown_mass[:, cell_count - 1, :], "narrow", 1)
    near_edges = extended(rim_cells, (("wide", 0),), block_dev)
    mine_upwind = lax.dynamic_slice_in_dim(upwind_blocks, owner_index * block_dev, block_dev)
    relative = (mine_upwind // block_dev - owner_index + 1 + wide_count) % wide_count
    edge_row = relative * block_dev + mine_upwind % block_dev
    far_edge = near_edges[edge_row]
    inflow = jnp.where(top_row, far_edge, rim_cells)
    moved_mass = advect(grown_mass, inflow, wind_speed)
    packed = moved_mass[slot_source] * slot_filled[:, None, None]
    haze_output_slots = lax.all_to_all(packed, "wide", split_axis=0, concat_axis=0, tiled=True)
    return (haze_output_slots, vapour_out)


def solution(mesh):
    in_specs = (
        P("wide", "narrow", None),
        P("wide", "narrow"),
        P("wide", "narrow"),
        P(),
        P(),
        P(),
        P(),
        P(),
        P(),
        P(),
    )
    out_specs = (P("wide", "narrow", None), P("wide", "narrow"))
    return jax.shard_map(local, mesh=mesh, in_specs=in_specs, out_specs=out_specs, check_vma=False)
```

profile of v0, /device:TPU:26, one launch (start us, length us, event | category | flops | bytes accessed | tf_op | source)
XLA Modules:
  0.0 103.3 jit_solution(7271616710510167857)
XLA Ops:
  0.6 0.0 copy-start
  0.7 2.1 %multiply_reduce_fusion = f32[64,32]{0,1:T(8,128)S(1)} fusion(f32[64,32,128]{2,1,0:T(8,128)} %param.10, f32[128]{0:T(128)} %param.13), kind=kLoop, calls=%fused_computation.15 | loop fusion | flops 522240 | bytes 1057280 | tf_op jit(solution)/shard_map/reduce_sum | solution.py:43
  2.8 0.7 divide_multiply_fusion
  3.5 0.0 copy-start.2
  3.5 2.2 %fusion.17 = f32[2048,8]{0,1:T(8,128)S(1)} fusion(f32[2048,128]{1,0:T(8,128)} %bitcast.21, f32[128,8]{0,1:T(8,128)} %param.14), kind=kOutput, calls=%fused_computation.49 | convolution fusion | flops 25165824 | bytes 1118208 | tf_op jit(solution)/shard_map/dot_general | solution.py:32
  5.7 0.0 copy-done.5
  5.7 1.0 convolution_multiply_fusion.1
  6.7 0.0 copy-start.7
  6.8 1.8 %fusion.18 = f32[2048,128]{1,0:T(8,128)S(1)} fusion(f32[2048,8]{0,1:T(8,128)S(1)} %convolution_multiply_fusion.1, f32[8,128]{1,0:T(8,128)S(1)} %copy-done), kind=kOutput, calls=%fused_computation.50 | convolution fusion | flops 25165824 | bytes 1118208 | tf_op jit(solution)/shard_map/dot_general | solution.py:36
  8.6 1.8 %fusion.1 = f32[2048,128]{1,0:T(8,128)S(1)} fusion(f32[2048,128]{1,0:T(8,128)S(1)} %fusion.18, f32[2048,128]{1,0:T(8,128)S(1)} %bitcast.23, f32[2048,8]{0,1:T(8,128)S(1)} %fusion.17, f32[8,128]{1,0:T(8,128)S(1)} %copy-done.6), kind=kOutput, calls=%fused_computation.6 | convolution fusion | flops 25952256 | bytes 3215360 | tf_op jit(solution)/shard_map/dot_general | solution.py:39
  10.4 1.2 %fusion.4 = f32[64,32,128]{2,0,1:T(8,128)S(1)} fusion(f32[64,32,128]{2,1,0:T(8,128)S(1)} %bitcast.24, f32[64,32,128]{2,1,0:T(8,128)S(1)} %copy-done.1, f32[64,32]{0,1:T(8,128)S(1)} %divide_multiply_fusion, f32[128]{0:T(128)S(1)} %copy-done.7), kind=kLoop, calls=%fused_computation.13 | loop fusion | flops 1048576 | bytes 3154432 | tf_op jit(solution)/shard_map/add | solution.py:46
  11.7 0.0 collective-permute-start
  11.7 0.5 broadcast.81
  12.2 0.7 reduce.3
  12.9 0.1 eq.22
  13.0 1.9 %convert_reduce_fusion = s32[64,64]{1,0:T(8,128)S(1)} fusion(s32[64,64]{1,0:T(8,128)S(1)} %eq.22, pred[64,64]{1,0:T(8,128)(4,1)S(1)} %iota_compare_fusion), kind=kLoop, calls=%fused_computation.8 | loop fusion | flops 1044480 | bytes 36864 | tf_op jit(solution)/shard_map/reduce_sum | solution.py:62
  14.9 0.1 reshape.35
  14.9 0.8 compare_select_fusion.2
  15.7 0.1 compare_select_fusion.1
  15.8 0.8 scatter_custom_fusion
  16.6 10.8 %collective-permute-start.2 = (f32[64,128]{1,0:T(8,128)S(1)}, f32[64,128]{1,0:T(8,128)S(1)}, u32[]{:S(2)}, u32[]{:S(2)}) collective-permute-start(f32[64,128]{1,0:T(8,128)S(1)} %collective-permute-done), channel_id=1, source_target_pairs={{8,0},{16,8},{24,16},{32,24},{40,32},{48,40},{56,48},{64,56},{72,6... | collective-permute-start | bytes 98312 | tf_op jit(solution)/shard_map/ppermute | solution.py:25
  27.5 1.9 %collective-permute-start.1 = (f32[64,128]{1,0:T(8,128)S(1)}, f32[64,128]{1,0:T(8,128)S(1)}, u32[]{:S(2)}, u32[]{:S(2)}) collective-permute-start(f32[64,128]{1,0:T(8,128)S(1)} %collective-permute-done), channel_id=1, source_target_pairs={{0,8},{8,16},{16,24},{24,32},{32,40},{40,48},{48,56},{56,64},{64,7... | collective-permute-start | bytes 98312 | tf_op jit(solution)/shard_map/ppermute | solution.py:22
  29.4 0.1 slice.13
  29.5 0.8 scatter_custom_fusion.1
  30.3 5.1 %collective-permute-done.1 = f32[64,128]{1,0:T(8,128)S(1)} collective-permute-done((f32[64,128]{1,0:T(8,128)S(1)}, f32[64,128]{1,0:T(8,128)S(1)}, u32[]{:S(2)}, u32[]{:S(2)}) %collective-permute-start.1) | collective-permute-done | bytes 32800 | tf_op jit(solution)/shard_map/ppermute | solution.py:22
  35.4 0.6 gather_fusion
  36.0 0.6 fusion.3
  36.6 0.6 copy.26
  37.3 0.8 gather_fusion.1
  38.1 0.2 broadcast_multiply_fusion
  38.3 63.8 %all_to_all.5 = f32[128,32,128]{2,1,0:T(8,128)S(1)} all-to-all(f32[128,32,128]{2,1,0:T(8,128)S(1)} %broadcast_multiply_fusion), channel_id=1, replica_groups=mesh['wide'=64,'narrow'=8] {'wide'}, dimensions={0} | all-to-all | bytes 4194304 | tf_op jit(solution)/shard_map/all_to_all | solution.py:103
  102.0 1.3 %copy.33 = f32[128,32,128]{2,1,0:T(8,128)} copy(f32[128,32,128]{2,1,0:T(8,128)S(1)} %all_to_all.5) | data formatting | bytes 4194304
  (23 shorter events, 0.1 us)
Async XLA Ops:
  0.6 6.1 %copy-start = (f32[8,128]{1,0:T(8,128)S(1)}, f32[8,128]{1,0:T(8,128)}, u32[]{:S(2)}) copy-start(f32[8,128]{1,0:T(8,128)} %param.16) | copy-start | bytes 12292
  0.6 5.1 %copy-start.1 = (f32[64,32,128]{2,1,0:T(8,128)S(1)}, f32[64,32,128]{2,1,0:T(8,128)}, u32[]{:S(2)}) copy-start(f32[64,32,128]{2,1,0:T(8,128)} %param.10) | copy-start | bytes 3145732
  0.7 5.1 %copy-start.5 = (f32[128,8]{0,1:T(8,128)S(1)}, f32[128,8]{0,1:T(8,128)}, u32[]{:S(2)}) copy-start(f32[128,8]{0,1:T(8,128)} %param.15) | copy-start | bytes 12292
  0.7 7.9 %copy-start.6 = (f32[8,128]{1,0:T(8,128)S(1)}, f32[8,128]{1,0:T(8,128)}, u32[]{:S(2)}) copy-start(f32[8,128]{1,0:T(8,128)} %param.17) | copy-start | bytes 12292
  3.5 6.9 %copy-start.2 = (f32[64,32]{0,1:T(8,128)}, f32[64,32]{0,1:T(8,128)S(1)}, u32[]{:S(2)}) copy-start(f32[64,32]{0,1:T(8,128)S(1)} %divide_multiply_fusion) | copy-start | bytes 24580
  6.7 3.7 %copy-start.7 = (f32[128]{0:T(128)S(1)}, f32[128]{0:T(128)}, u32[]{:S(2)}) copy-start(f32[128]{0:T(128)} %param.13) | copy-start | bytes 1540
  10.4 1.8 %copy-start.3 = (s32[4096,1]{0,1:T(1,128)S(1)}, s32[4096,1]{0,1:T(1,128)}, u32[]{:S(2)}) copy-start(s32[4096,1]{0,1:T(1,128)} %param.18) | copy-start | bytes 49156
  11.7 24.4 %copy-start.4 = (f32[64,32]{0,1:T(8,128)S(1)}, f32[64,32]{0,1:T(8,128)}, u32[]{:S(2)}) copy-start(f32[64,32]{0,1:T(8,128)} %param.11) | copy-start | bytes 24580
  11.7 4.9 %collective-permute-start = (f32[64,128]{1,0:T(8,128)S(1)}, f32[64,128]{1,0:T(8,128)S(1)}, u32[]{:S(2)}, u32[]{:S(2)}) collective-permute-start(f32[64,128]{1,0:T(8,128)S(1)} %slice_bitcast_fusion), channel_id=1, source_target_pairs={{7,0},{0,1},{1,2},{2,3},{3,4},{4,5},{5,6},{6,7},{15,8},{8,9},{9,10... | collective-permute-start | bytes 98312 | tf_op jit(solution)/shard_map/ppermute | solution.py:13
  16.6 13.7 %collective-permute-start.2 = (f32[64,128]{1,0:T(8,128)S(1)}, f32[64,128]{1,0:T(8,128)S(1)}, u32[]{:S(2)}, u32[]{:S(2)}) collective-permute-start(f32[64,128]{1,0:T(8,128)S(1)} %collective-permute-done), channel_id=1, source_target_pairs={{8,0},{16,8},{24,16},{32,24},{40,32},{48,40},{56,48},{64,56},{72,6... | collective-permute-start | bytes 98312 | tf_op jit(solution)/shard_map/ppermute | solution.py:25
  27.5 7.9 %collective-permute-start.1 = (f32[64,128]{1,0:T(8,128)S(1)}, f32[64,128]{1,0:T(8,128)S(1)}, u32[]{:S(2)}, u32[]{:S(2)}) collective-permute-start(f32[64,128]{1,0:T(8,128)S(1)} %collective-permute-done), channel_id=1, source_target_pairs={{0,8},{8,16},{16,24},{24,32},{32,40},{40,48},{48,56},{56,64},{64,7... | collective-permute-start | bytes 98312 | tf_op jit(solution)/shard_map/ppermute | solution.py:22
where the time goes:
time: 104 us; the launch traced here: 103 us
  blocking collectives  63.8 us (61%)
  starting transfers between devices  12.8 us (12%)
  other arithmetic  8.27 us (8%)
  matrix products  6.82 us (7%)
  local copies, waits for them, and re-layouts  5.7 us (5%)
  waiting for transfers between devices  5.09 us (5%)
    all_to_all x1, blocking collectives, local(): lax.all_to_all(packed, 'wide', split_axis=0, concat_axis=0, tiled=True)  63.8 us
    ppermute x1, starting transfers between devices, extended(): lax.ppermute(lax.slice_in_dim(block, 0, width, axis=dim), axis, backward)  10.8 us
    ppermute x1, waiting for transfers between devices, extended(): lax.ppermute(lax.slice_in_dim(block, block.shape[dim] - width, None, axis...  5.08 us
    dot_general x1, matrix products, microphysics(): jnp.dot(flat_rows, coag_left, precision=PRECISE, preferred_element_type=j...  2.21 us
    reduce_sum x1, other arithmetic, microphysics(): mean_take = jnp.mean(haze_bin_mass * uptake_rates, axis=-1)  2.08 us
  transfers between devices with their start and end apart: 3, of which 1 were waited for; matrix products, arithmetic and copies ran while one was open for 6% of the time, Pallas kernels for 0%

commit v1 on v0

v1 whole, which is shorter than its diff:
```python
import jax
import jax.numpy as jnp
from jax import lax
from jax.experimental import pallas as pl
from jax.experimental.pallas import tpu as pltpu
from jax.sharding import PartitionSpec as P

HIGHEST = lax.Precision.HIGHEST
STEP_DT = 0.25
F32 = jnp.float32
I32 = jnp.int32
VMEM = pltpu.VMEM


def precise_dot(a, b):
    return jnp.dot(a, b, precision=HIGHEST, preferred_element_type=F32)


def column_rows(table, column, rows, lanes):
    return jnp.broadcast_to(table[:, column : column + 1], (rows, lanes))


def fill_weights(first_rows, first_weights, second_weights, left, right, uptake, gain, loss):
    rank, bins = left.shape
    first_rows[...] = jnp.zeros_like(first_rows)
    first_rows[0:rank, :] = left
    first_rows[rank : 2 * rank, :] = left
    first_rows[bins : bins + rank, :] = right
    first_rows[2 * bins :, :] = jnp.broadcast_to(uptake * (1.0 / bins), (bins, bins))
    for k in range(3):
        first_weights[:, k * bins : (k + 1) * bins] = first_rows[k * bins : (k + 1) * bins, :].T
    second_weights[...] = jnp.zeros_like(second_weights)
    second_weights[0:rank, 0:bins] = STEP_DT * gain
    second_weights[rank : 2 * rank, bins:] = STEP_DT * loss


def weight_scratch(bins):
    return [
        pltpu.VMEM((3 * bins, bins), F32),
        pltpu.VMEM((bins, 3 * bins), F32),
        pltpu.VMEM((bins, 2 * bins), F32),
    ]


def rows_of_lanes(row, lanes):
    count = row.shape[1]
    shape = (count, count)
    eye = lax.broadcasted_iota(I32, shape, 0) == lax.broadcasted_iota(I32, shape, 1)
    spread = jnp.where(eye, jnp.broadcast_to(row, shape), 0.0)
    return precise_dot(spread, jnp.ones((count, lanes), F32))


def grow(x, vapour_rows, first_weights, second_weights, uptake, rank):
    rows, bins = x.shape
    lane = lax.broadcasted_iota(I32, (rows, bins), 1)
    one_lanes = jnp.where((lane >= rank) & (lane < 2 * rank), 1.0, 0.0).astype(F32)
    proj = precise_dot(x, first_weights[...])
    product = proj[:, :bins] * (proj[:, bins : 2 * bins] + one_lanes)
    rate = precise_dot(product, second_weights[...])
    taken = vapour_rows * (1.0 / (1.0 + vapour_rows * proj[:, 2 * bins :]))
    grown = x + (rate[:, :bins] - x * rate[:, bins:]) + taken * uptake * x
    return grown, taken


def rim_kernel(
    haze_hbm,
    vapour_ref,
    uptake_ref,
    left_ref,
    right_ref,
    gain_ref,
    loss_ref,
    rim_ref,
    rows_buf,
    first_rows,
    first_weights,
    second_weights,
    sem,
):
    cells = haze_hbm.shape[1]
    copy = pltpu.make_async_copy(haze_hbm.at[:, cells - 1, :], rows_buf, sem)
    copy.start()
    uptake = uptake_ref[...]
    weights = (left_ref[...], right_ref[...], uptake, gain_ref[...], loss_ref[...])
    fill_weights(first_rows, first_weights, second_weights, *weights)
    vapour_rows = rows_of_lanes(vapour_ref[cells - 1 : cells, :], rows_buf.shape[1])
    copy.wait()
    rim_ref[...], _ = grow(
        rows_buf[...], vapour_rows, first_weights, second_weights, uptake, left_ref.shape[0]
    )


def pack_kernel(
    haze_hbm,
    wind_ref,
    vapour_ref,
    uptake_ref,
    left_ref,
    right_ref,
    gain_ref,
    loss_ref,
    targets_hbm,
    upwind_hbm,
    packed_ref,
    top_ref,
    wind_top_ref,
    slot_ref,
    source_ref,
    haze_buf,
    first_rows,
    first_weights,
    second_weights,
    window,
    upwind_window,
    used,
    haze_sems,
    window_sems,
):
    blocks, cells, bins = haze_buf.shape
    rank = left_ref.shape[0]
    group = 8
    rows = group * cells
    wide_count = lax.axis_size("wide")
    owner = lax.axis_index("wide")
    first = lax.axis_index("narrow") == 0
    start = owner * blocks
    base = pl.multiple_of((start // 128) * 128, 128)
    far_base = pl.multiple_of((start // 1024) * 1024, 1024)
    window_copies = [
        pltpu.make_async_copy(targets_hbm.at[:, pl.ds(base, 128)], window, window_sems.at[0]),
        pltpu.make_async_copy(
            upwind_hbm.at[pl.ds(far_base, 1024)], upwind_window, window_sems.at[1]
        ),
    ]
    for copy in window_copies:
        copy.start()
    copies = []
    for g in range(blocks // group):
        part = pl.ds(g * group, group)
        copy = pltpu.make_async_copy(haze_hbm.at[part], haze_buf.at[part], haze_sems.at[g])
        copy.start()
        copies.append(copy)
    packed_ref[...] = jnp.zeros_like(packed_ref)
    for t in range(used.shape[0]):
        used[t] = 0
    uptake = uptake_ref[...]
    weights = (left_ref[...], right_ref[...], uptake, gain_ref[...], loss_ref[...])
    fill_weights(first_rows, first_weights, second_weights, *weights)
    top_row = lax.broadcasted_iota(I32, (rows, bins), 0) % cells == 0
    wind = wind_ref[...]
    vapour = vapour_ref[...]
    wind_top_ref[...] = rows_of_lanes(wind_ref[0:1, :], bins)
    for copy in window_copies:
        copy.wait()
    for g in range(blocks // group):
        copies[g].wait()
        x = haze_buf[g * group : (g + 1) * group].reshape(rows, bins)
        ids = range(g * group, (g + 1) * group)
        vapour_rows = jnp.concatenate([column_rows(vapour, b, cells, bins) for b in ids], 0)
        wind_rows = jnp.concatenate([column_rows(wind, b, cells, bins) for b in ids], 0)
        grown, _ = grow(x, vapour_rows, first_weights, second_weights, uptake, rank)
        upwind = jnp.where(top_row, 0.0, pltpu.roll(grown, 1, 0))
        moved = grown - wind_rows * (grown - upwind)
        for j, b in enumerate(ids):
            at = j * cells
            target = window[0, start - base + b]
            rank_within = used[target]
            used[target] = rank_within + 1
            slot = target * 2 + rank_within
            slot_ref[b] = slot
            packed_ref[slot] = moved[at : at + cells, :]
            top_ref[b : b + 1, :] = moved[at : at + 1, :]
            source = upwind_window[start - far_base + b]
            relative = lax.rem(source // blocks - owner + 1 + wide_count, wide_count)
            far = relative * blocks + lax.rem(source, blocks)
            source_ref[b] = jnp.where(first, far, blocks + b)


def inflow_kernel(
    packed_in,
    top_ref,
    wind_top_ref,
    same_ref,
    low_ref,
    high_ref,
    slot_ref,
    source_ref,
    packed_hbm,
    near,
    inflow,
    sem,
):
    blocks, bins = same_ref.shape
    near[0:blocks, :] = low_ref[...]
    near[blocks : 2 * blocks, :] = same_ref[...]
    near[2 * blocks :, :] = high_ref[...]
    for b in range(blocks):
        inflow[b : b + 1, :] = near[pl.ds(source_ref[b], 1), :]
    inflow[...] = top_ref[...] + wind_top_ref[...] * inflow[...]
    for b in range(blocks):
        pltpu.make_async_copy(inflow.at[b], packed_hbm.at[slot_ref[b], 0], sem).start()
    pltpu.make_async_copy(inflow, packed_hbm.at[pl.ds(0, blocks), 0, :], sem).wait()


def vapour_kernel(haze_ref, vapour_ref, uptake_ref, vapour_out_ref):
    blocks, cells, bins = haze_ref.shape
    vapour = vapour_ref[...]
    weights = jnp.broadcast_to(uptake_ref[...] * (1.0 / bins), (bins, bins)).T
    lane = lax.broadcasted_iota(I32, (cells, blocks), 1)
    out = jnp.zeros((cells, blocks), F32)
    for g in range(0, blocks, 8):
        mean_take = precise_dot(haze_ref[g : g + 8].reshape(8 * cells, bins), weights)
        for j in range(8):
            part = mean_take[j * cells : (j + 1) * cells, :blocks]
            out = jnp.where(lane == g + j, part, out)
    vapour_out_ref[...] = vapour * (1.0 / (1.0 + vapour * out))


def whole(space=VMEM):
    return pl.BlockSpec(memory_space=space)


def cost(flops, moved):
    return pl.CostEstimate(flops=flops, bytes_accessed=moved, transcendentals=0)


def local(
    haze_bin_mass,
    wind_speed,
    vapour,
    uptake_rates,
    coag_left,
    coag_right,
    coag_gain,
    coag_loss,
    targets,
    upwind_blocks,
):
    wide_count = lax.axis_size("wide")
    narrow_count = lax.axis_size("narrow")
    blocks, cells, bins = haze_bin_mass.shape
    slots = 2 * wide_count
    vapour_t = vapour.T
    uptake_row = uptake_rates[None, :]
    rates = (uptake_row, coag_left.T, coag_right.T, coag_gain, coag_loss)
    rim_type = jax.ShapeDtypeStruct((blocks, bins), F32)
    packed_type = jax.ShapeDtypeStruct((slots, cells, bins), F32)
    ids_type = jax.ShapeDtypeStruct((blocks,), I32)
    rim = pl.pallas_call(
        rim_kernel,
        out_shape=rim_type,
        in_specs=[whole(pl.ANY)] + [whole()] * 6,
        out_specs=whole(),
        scratch_shapes=[
            pltpu.VMEM((blocks, bins), F32),
            *weight_scratch(bins),
            pltpu.SemaphoreType.DMA,
        ],
        cost_estimate=cost(10000000, 100000),
    )(haze_bin_mass, vapour_t, *rates)
    last = narrow_count - 1
    both = ("wide", "narrow")
    along = [
        (w * narrow_count + n, w * narrow_count + (n + 1) % narrow_count)
        for w in range(wide_count)
        for n in range(narrow_count)
    ]
    up = [
        (w * narrow_count + last, ((w + 1) % wide_count) * narrow_count)
        for w in range(wide_count)
    ]
    down = [
        (w * narrow_count + last, ((w - 1) % wide_count) * narrow_count)
        for w in range(wide_count)
    ]
    low = lax.ppermute(rim, both, up)
    high = lax.ppermute(rim, both, down)
    same = lax.ppermute(rim, both, along)
    packed, top, wind_top, slot, source = pl.pallas_call(
        pack_kernel,
        out_shape=(packed_type, rim_type, rim_type, ids_type, ids_type),
        in_specs=[whole(pl.ANY)] + [whole()] * 7 + [whole(pl.ANY)] * 2,
        out_specs=(whole(),) * 3 + (whole(pltpu.SMEM),) * 2,
        scratch_shapes=[
            pltpu.VMEM((blocks, cells, bins), F32),
            *weight_scratch(bins),
            pltpu.SMEM((1, 128), I32),
            pltpu.SMEM((1024,), I32),
            pltpu.SMEM((wide_count,), I32),
            pltpu.SemaphoreType.DMA((blocks // 8,)),
            pltpu.SemaphoreType.DMA((2,)),
        ],
        cost_estimate=cost(800000000, 4000000),
        compiler_params=pltpu.CompilerParams(vmem_limit_bytes=67043328),
    )(haze_bin_mass, wind_speed.T, vapour_t, *rates, targets.T, upwind_blocks)
    packed = pl.pallas_call(
        inflow_kernel,
        out_shape=packed_type,
        in_specs=[whole(pl.ANY)] + [whole()] * 5 + [whole(pltpu.SMEM)] * 2,
        out_specs=whole(pl.ANY),
        scratch_shapes=[
            pltpu.VMEM((3 * blocks, bins), F32),
            pltpu.VMEM((blocks, bins), F32),
            pltpu.SemaphoreType.DMA,
        ],
        input_output_aliases={0: 0},
        cost_estimate=cost(100000, 300000),
    )(packed, top, wind_top, same, low, high, slot, source)
    haze_output_slots = lax.all_to_all(packed, "wide", split_axis=0, concat_axis=0, tiled=True)
    vapour_out = pl.pallas_call(
        vapour_kernel,
        out_shape=jax.ShapeDtypeStruct((cells, blocks), F32),
        in_specs=[whole()] * 3,
        out_specs=whole(),
        cost_estimate=cost(400000000, 1000000),
        compiler_params=pltpu.CompilerParams(vmem_limit_bytes=67043328),
    )(haze_bin_mass, vapour_t, uptake_row)
    return (haze_output_slots, vapour_out.T)


def solution(mesh):
    in_specs = (
        P("wide", "narrow", None),
        P("wide", "narrow"),
        P("wide", "narrow"),
        P(),
        P(),
        P(),
        P(),
        P(),
        P(),
        P(),
    )
    out_specs = (P("wide", "narrow", None), P("wide", "narrow"))
    return jax.shard_map(local, mesh=mesh, in_specs=in_specs, out_specs=out_specs, check_vma=False)
```

time: 104 us -> 99.2 us (0.954)
  the two profiles are of different devices: /device:TPU:26 before, /device:TPU:27 now
where the time goes in v1:
time: 99.2 us; the launch traced here: 98.6 us
  waiting for transfers between devices  56.1 us (57%)
  starting transfers between devices  20.3 us (20%)
  Pallas kernels  18.5 us (19%)
  local copies, waits for them, and re-layouts  3.08 us (3%)
    all_to_all x1, waiting for transfers between devices, local(): lax.all_to_all(packed, 'wide', split_axis=0, concat_axis=0, tiled=True)  56.1 us
    all_to_all x1, starting transfers between devices, local(): lax.all_to_all(packed, 'wide', split_axis=0, concat_axis=0, tiled=True)  16 us
    pallas_call x1, Pallas kernels, local(): pl.pallas_call(pack_kernel, out_shape=(packed_type, rim_type, rim_type, i...  11.4 us
    unnamed x1, local copies, waits for them, and re-layouts  3.08 us
    pallas_call x1, Pallas kernels, local(): pl.pallas_call(vapour_kernel, out_shape=jax.ShapeDtypeStruct((cells, bloc...  2.87 us
    pallas_call x1, Pallas kernels, local(): pl.pallas_call(rim_kernel, out_shape=rim_type, in_specs=[whole(pl.ANY)] +...  2.59 us
  transfers between devices with their start and end apart: 4, of which 1 were waited for; matrix products, arithmetic and copies ran while one was open for 0% of the time, Pallas kernels for 14%

profile of v1, /device:TPU:27, one launch (start us, length us, event | category | flops | bytes accessed | tf_op | source)
XLA Modules:
  0.0 98.6 jit_solution(3943383470802736904)
XLA Ops:
  0.6 2.6 %shard_map.114 = f32[64,128]{1,0:T(8,128)} custom-call(f32[64,32,128]{2,1,0:T(8,128)} %haze_ref.1, f32[32,64]{1,0:T(8,128)} %bitcast.7, f32[1,128]{1,0:T(1,128)} %bitcast.14, f32[8,128]{1,0:T(8,128)} %bitcast.10, f32[8,128]{1,0:T(8,128)} %bitcast.12, f32[8,128]{1,0:T(8,128)} %gain_ref.3, f32[8,128]{1,0:T(8,128)} %loss_ref.3), custom_call_target="tpu_custom_call" | custom-call | flops 10000000 | bytes 100000 | tf_op jit(solution)/shard_map/pallas_call | solution.py:249
  3.2 1.8 %collective-permute-start = (f32[64,128]{1,0:T(8,128)}, f32[64,128]{1,0:T(8,128)}, u32[]{:S(2)}, u32[]{:S(2)}) collective-permute-start(f32[64,128]{1,0:T(8,128)} %shard_map.114), channel_id=1, source_target_pairs={{0,1},{1,2},{2,3},{3,4},{4,5},{5,6},{6,7},{7,0},{8,9},{9,10},{10,1... | collective-permute-start | bytes 98312 | tf_op jit(solution)/shard_map/ppermute | solution.py:278
  5.0 1.3 %collective-permute-start.1 = (f32[64,128]{1,0:T(8,128)}, f32[64,128]{1,0:T(8,128)}, u32[]{:S(2)}, u32[]{:S(2)}) collective-permute-start(f32[64,128]{1,0:T(8,128)} %shard_map.114), channel_id=1, source_target_pairs={{7,8},{15,16},{23,24},{31,32},{39,40},{47,48},{55,56},{63,64},{71,... | collective-permute-start | bytes 98312 | tf_op jit(solution)/shard_map/ppermute | solution.py:276
  6.3 1.2 %collective-permute-start.2 = (f32[64,128]{1,0:T(8,128)}, f32[64,128]{1,0:T(8,128)}, u32[]{:S(2)}, u32[]{:S(2)}) collective-permute-start(f32[64,128]{1,0:T(8,128)} %shard_map.114), channel_id=1, source_target_pairs={{7,504},{15,0},{23,8},{31,16},{39,24},{47,32},{55,40},{63,48},{71,... | collective-permute-start | bytes 98312 | tf_op jit(solution)/shard_map/ppermute | solution.py:277
  7.5 11.4 %shard_map.113 = (f32[128,32,128]{2,1,0:T(8,128)}, f32[64,128]{1,0:T(8,128)}, f32[64,128]{1,0:T(8,128)}, s32[64]{0:T(128)}, s32[64]{0:T(128)}) custom-call(f32[64,32,128]{2,1,0:T(8,128)} %haze_ref.1, f32[32,64]{1,0:T(8,128)} %bitcast.17, f32[32,64]{1,0:T(8,128)} %bitcast.8, f32[1,128]{1,0:T(1,128)} %bitcast.15, f32[8,128]{1,0:T(8,128)} %bitcast.11, ...), custom_call_target="tpu_custom_call" | custom-call | flops 800000000 | bytes 4000000 | tf_op jit(solution)/shard_map/pallas_call | solution.py:279
  18.9 0.0 collective-permute-done.same_ref
  18.9 0.0 collective-permute-done.1.low_ref
  18.9 0.0 collective-permute-done.2.high_ref
  18.9 1.7 %shard_map.115 = f32[128,32,128]{2,1,0:T(8,128)} custom-call(f32[128,32,128]{2,1,0:T(8,128)} %get-tuple-element.7.packed_in, f32[64,128]{1,0:T(8,128)} %get-tuple-element.8.top_ref, f32[64,128]{1,0:T(8,128)} %get-tuple-element.9.wind_top_ref, f32[64,128]{1,0:T(8,128)} %collective-permute-done.same_ref, ...), custom_call_target="tpu_custom_call", output_to_operand_aliasing={{}: (0, {})} | custom-call | flops 100000 | bytes 300000 | tf_op jit(solution)/shard_map/pallas_call | solution.py:296
  20.6 16.0 %all-to-all-start = ((f32[128,32,128]{2,1,0:T(8,128)}), f32[128,32,128]{2,1,0:T(8,128)}, u32[]{:S(2)}, u32[]{:S(2)}) async-start(f32[128,32,128]{2,1,0:T(8,128)} %shard_map.115), calls=%async_computation | async-start | bytes 4194304 | tf_op jit(solution)/shard_map/all_to_all | solution.py:309
  36.6 2.9 %shard_map.116 = f32[32,64]{1,0:T(8,128)} custom-call(f32[64,32,128]{2,1,0:T(8,128)} %haze_ref.1, f32[32,64]{1,0:T(8,128)} %bitcast.9, f32[1,128]{1,0:T(1,128)} %bitcast.16), custom_call_target="tpu_custom_call" | custom-call | flops 400000000 | bytes 1000000 | tf_op jit(solution)/shard_map/pallas_call | solution.py:310
  39.5 56.1 %all-to-all-done = f32[128,32,128]{2,1,0:T(8,128)} async-done(((f32[128,32,128]{2,1,0:T(8,128)}), f32[128,32,128]{2,1,0:T(8,128)}, u32[]{:S(2)}, u32[]{:S(2)}) %all-to-all-start) | async-done | bytes 2097184 | tf_op jit(solution)/shard_map/all_to_all | solution.py:309
  95.6 3.1 %copy.15 = f32[128,32,128]{2,1,0:T(8,128)} copy(f32[128,32,128]{2,1,0:T(8,128)} %all-to-all-done) | data formatting | bytes 4194304
Async XLA Ops:
  3.2 15.7 %collective-permute-start = (f32[64,128]{1,0:T(8,128)}, f32[64,128]{1,0:T(8,128)}, u32[]{:S(2)}, u32[]{:S(2)}) collective-permute-start(f32[64,128]{1,0:T(8,128)} %shard_map.114), channel_id=1, source_target_pairs={{0,1},{1,2},{2,3},{3,4},{4,5},{5,6},{6,7},{7,0},{8,9},{9,10},{10,1... | collective-permute-start | bytes 98312 | tf_op jit(solution)/shard_map/ppermute | solution.py:278
  5.0 13.9 %collective-permute-start.1 = (f32[64,128]{1,0:T(8,128)}, f32[64,128]{1,0:T(8,128)}, u32[]{:S(2)}, u32[]{:S(2)}) collective-permute-start(f32[64,128]{1,0:T(8,128)} %shard_map.114), channel_id=1, source_target_pairs={{7,8},{15,16},{23,24},{31,32},{39,40},{47,48},{55,56},{63,64},{71,... | collective-permute-start | bytes 98312 | tf_op jit(solution)/shard_map/ppermute | solution.py:276
  6.3 12.6 %collective-permute-start.2 = (f32[64,128]{1,0:T(8,128)}, f32[64,128]{1,0:T(8,128)}, u32[]{:S(2)}, u32[]{:S(2)}) collective-permute-start(f32[64,128]{1,0:T(8,128)} %shard_map.114), channel_id=1, source_target_pairs={{7,504},{15,0},{23,8},{31,16},{39,24},{47,32},{55,40},{63,48},{71,... | collective-permute-start | bytes 98312 | tf_op jit(solution)/shard_map/ppermute | solution.py:277
  20.6 75.0 %all-to-all-start = ((f32[128,32,128]{2,1,0:T(8,128)}), f32[128,32,128]{2,1,0:T(8,128)}, u32[]{:S(2)}, u32[]{:S(2)}) async-start(f32[128,32,128]{2,1,0:T(8,128)} %shard_map.115), calls=%async_computation | async-start | bytes 4194304 | tf_op jit(solution)/shard_map/all_to_all | solution.py:309

commit v2 on v1

v2 whole, which is shorter than its diff:
```python
import jax
import jax.numpy as jnp
from jax import lax
from jax.experimental import pallas as pl
from jax.experimental.pallas import tpu as pltpu
from jax.sharding import PartitionSpec as P

HIGHEST = lax.Precision.HIGHEST
STEP_DT = 0.25
F32 = jnp.float32
BF16 = jnp.bfloat16
I32 = jnp.int32
VMEM = pltpu.VMEM
SEGMENT = 32
TAKE_LANE = 24
COLUMNS = 8


def precise_dot(a, b):
    return jnp.dot(a, b, precision=HIGHEST, preferred_element_type=F32)


def split(x):
    high = x.astype(BF16)
    return high, (x - high.astype(F32)).astype(BF16)


def column_rows(table, column, rows, lanes):
    return jnp.broadcast_to(table[:, column : column + 1], (rows, lanes))


def rows_of_lanes(row, lanes):
    count = row.shape[1]
    shape = (count, count)
    eye = lax.broadcasted_iota(I32, shape, 0) == lax.broadcasted_iota(I32, shape, 1)
    spread = jnp.where(eye, jnp.broadcast_to(row, shape), 0.0)
    return precise_dot(spread, jnp.ones((count, lanes), F32))


def fill_weights(columns, second, first_both, first_low, second_ref, left, right, uptake, gain, loss):
    rank, bins = left.shape
    columns[...] = jnp.zeros_like(columns)
    for at in range(0, 3 * SEGMENT, SEGMENT):
        columns[at : at + rank, :] = left
        columns[at + rank : at + 2 * rank, :] = left
        columns[at + TAKE_LANE : at + TAKE_LANE + 1, :] = uptake * (1.0 / bins)
        columns[bins + at : bins + at + rank, :] = right
    for k in range(0, 2 * bins, bins):
        high, low = split(columns[k : k + bins, :].T)
        first_both[0:bins, k : k + bins] = high
        first_both[bins:, k : k + bins] = high
        first_low[:, k : k + bins] = low
    second[...] = jnp.zeros_like(second)
    second[0:rank, 0:bins] = STEP_DT * gain
    second[rank : 2 * rank, bins:] = STEP_DT * loss
    second[TAKE_LANE : TAKE_LANE + 1, bins:] = -uptake
    high, low = split(second[...])
    second_ref[0:SEGMENT, :] = high
    second_ref[SEGMENT : 2 * SEGMENT, :] = low
    second_ref[2 * SEGMENT : 3 * SEGMENT, :] = high
    second_ref[3 * SEGMENT :, :] = jnp.zeros_like(high)


def grow(x, vapour_rows, first_both, first_low, second, rank):
    rows, bins = x.shape
    lane = lax.broadcasted_iota(I32, (rows, bins), 1)
    place = lane & (SEGMENT - 1)
    one_lanes = jnp.where((place >= rank) & (place < 2 * rank), 1.0, 0.0).astype(F32)
    high, low = split(x)
    proj = jnp.dot(jnp.concatenate([high, low], 1), first_both[...], preferred_element_type=F32)
    proj = proj + jnp.dot(high, first_low[...], preferred_element_type=F32)
    left, right = proj[:, :bins], proj[:, bins:]
    taken = vapour_rows / (1.0 + vapour_rows * left)
    product = jnp.where(place == TAKE_LANE, taken, left * (right + one_lanes))
    product = jnp.where(lane < 3 * SEGMENT, product, 0.0)
    high, low = split(product)
    parts = jnp.where(lane < 2 * SEGMENT, high.astype(F32), low.astype(F32)).astype(BF16)
    rate = jnp.dot(parts, second[...], preferred_element_type=F32)
    return x + (rate[:, :bins] - x * rate[:, bins:])


def pack_kernel(
    haze_hbm,
    wind_ref,
    vapour_ref,
    uptake_ref,
    left_ref,
    right_ref,
    gain_ref,
    loss_ref,
    targets_hbm,
    upwind_hbm,
    packed_ref,
    top_ref,
    wind_top_ref,
    first_both,
    first_low,
    second,
    slot_ref,
    source_ref,
    haze_buf,
    columns,
    second_buf,
    window,
    upwind_window,
    used,
    haze_sems,
    window_sems,
):
    blocks, cells, bins = haze_buf.shape
    rank = left_ref.shape[0]
    group = 8
    rows = group * cells
    wide_count = lax.axis_size("wide")
    owner = lax.axis_index("wide")
    first = lax.axis_index("narrow") == 0
    start = owner * blocks
    base = pl.multiple_of((start // 128) * 128, 128)
    far_base = pl.multiple_of((start // 1024) * 1024, 1024)
    window_copies = [
        pltpu.make_async_copy(targets_hbm.at[:, pl.ds(base, 128)], window, window_sems.at[0]),
        pltpu.make_async_copy(
            upwind_hbm.at[pl.ds(far_base, 1024)], upwind_window, window_sems.at[1]
        ),
    ]
    for copy in window_copies:
        copy.start()
    copies = []
    for g in range(blocks // group):
        part = pl.ds(g * group, group)
        copy = pltpu.make_async_copy(haze_hbm.at[part], haze_buf.at[part], haze_sems.at[g])
        copy.start()
        copies.append(copy)
    packed_ref[...] = jnp.zeros_like(packed_ref)
    for t in range(used.shape[0]):
        used[t] = 0
    fill_weights(
        columns,
        second_buf,
        first_both,
        first_low,
        second,
        left_ref[...],
        right_ref[...],
        uptake_ref[...],
        gain_ref[...],
        loss_ref[...],
    )
    top_row = lax.broadcasted_iota(I32, (rows, bins), 0) % cells == 0
    wind = wind_ref[...]
    vapour = vapour_ref[...]
    wind_top_ref[...] = rows_of_lanes(wind_ref[0:1, :], bins)
    for copy in window_copies:
        copy.wait()
    block_bits = blocks.bit_length() - 1
    column_bits = COLUMNS.bit_length() - 1
    line_bits = (wide_count // COLUMNS).bit_length() - 1
    for g in range(blocks // group):
        copies[g].wait()
        x = haze_buf[g * group : (g + 1) * group].reshape(rows, bins)
        ids = range(g * group, (g + 1) * group)
        vapour_rows = jnp.concatenate([column_rows(vapour, b, cells, bins) for b in ids], 0)
        wind_rows = jnp.concatenate([column_rows(wind, b, cells, bins) for b in ids], 0)
        grown = grow(x, vapour_rows, first_both, first_low, second, rank)
        upwind = jnp.where(top_row, 0.0, pltpu.roll(grown, 1, 0))
        moved = grown - wind_rows * (grown - upwind)
        for j, b in enumerate(ids):
            at = j * cells
            target = window[0, start - base + b]
            rank_within = used[target]
            used[target] = rank_within + 1
            position = ((target & (COLUMNS - 1)) << line_bits) + (target >> column_bits)
            slot = position * 2 + rank_within
            slot_ref[b] = slot
            packed_ref[slot] = moved[at : at + cells, :]
            top_ref[b : b + 1, :] = moved[at : at + 1, :]
            source = upwind_window[start - far_base + b]
            relative = ((source >> block_bits) - owner + 1 + wide_count) & (wide_count - 1)
            far = (relative << block_bits) + (source & (blocks - 1))
            source_ref[b] = jnp.where(first, far, blocks + b)


def inflow_kernel(
    packed_in,
    top_ref,
    wind_top_ref,
    same_ref,
    low_ref,
    high_ref,
    first_both,
    first_low,
    second,
    slot_ref,
    source_ref,
    packed_hbm,
    near,
    inflow,
    rows_buf,
    sem,
    *,
    rank,
):
    blocks, bins = top_ref.shape
    near[0:blocks, :] = low_ref[...]
    near[blocks : 2 * blocks, :] = same_ref[...]
    near[2 * blocks :, :] = high_ref[...]
    for b in range(blocks):
        rows_buf[b : b + 1, :] = near[pl.ds(source_ref[b], 1), :]
    grown = grow(rows_buf[:, :bins], rows_buf[:, bins:], first_both, first_low, second, rank)
    inflow[...] = top_ref[...] + wind_top_ref[...] * grown
    for b in range(blocks):
        pltpu.make_async_copy(inflow.at[b], packed_hbm.at[slot_ref[b], 0], sem).start()
    pltpu.make_async_copy(inflow, packed_hbm.at[pl.ds(0, blocks), 0, :], sem).wait()


def vapour_kernel(haze_ref, vapour_ref, uptake_ref, vapour_out_ref):
    blocks, cells, bins = haze_ref.shape
    vapour = vapour_ref[...]
    weights = jnp.broadcast_to(uptake_ref[...] * (1.0 / bins), (bins, bins)).T
    lane = lax.broadcasted_iota(I32, (cells, blocks), 1)
    out = jnp.zeros((cells, blocks), F32)
    for g in range(0, blocks, 8):
        mean_take = precise_dot(haze_ref[g : g + 8].reshape(8 * cells, bins), weights)
        for j in range(8):
            part = mean_take[j * cells : (j + 1) * cells, :blocks]
            out = jnp.where(lane == g + j, part, out)
    vapour_out_ref[...] = vapour * (1.0 / (1.0 + vapour * out))


def whole(space=VMEM):
    return pl.BlockSpec(memory_space=space)


def cost(flops, moved):
    return pl.CostEstimate(flops=flops, bytes_accessed=moved, transcendentals=0)


def local(
    haze_bin_mass,
    wind_speed,
    vapour,
    uptake_rates,
    coag_left,
    coag_right,
    coag_gain,
    coag_loss,
    targets,
    upwind_blocks,
):
    wide_count = lax.axis_size("wide")
    narrow_count = lax.axis_size("narrow")
    blocks, cells, bins = haze_bin_mass.shape
    slots = 2 * wide_count
    vapour_t = vapour.T
    uptake_row = uptake_rates[None, :]
    rates = (uptake_row, coag_left.T, coag_right.T, coag_gain, coag_loss)
    rim = jnp.concatenate(
        [haze_bin_mass[:, cells - 1, :], jnp.broadcast_to(vapour[:, cells - 1 :], (blocks, bins))], 1
    )

    def passed(distance):
        route = [
            (
                w * narrow_count + n,
                ((w + distance) % wide_count) * narrow_count + (n + 1) % narrow_count,
            )
            for w in range(wide_count)
            for n in range(narrow_count)
        ]
        return lax.ppermute(rim, ("wide", "narrow"), route)

    same, low, high = passed(0), passed(1), passed(-1)

    def shape(*dims, kind=F32):
        return jax.ShapeDtypeStruct(dims, kind)

    packed_type = shape(slots, cells, bins)
    packed, top, wind_top, first_both, first_low, second, slot, source = pl.pallas_call(
        pack_kernel,
        out_shape=(
            packed_type,
            shape(blocks, bins),
            shape(blocks, bins),
            shape(2 * bins, 2 * bins, kind=BF16),
            shape(bins, 2 * bins, kind=BF16),
            shape(bins, 2 * bins, kind=BF16),
            shape(blocks, kind=I32),
            shape(blocks, kind=I32),
        ),
        in_specs=[whole(pl.ANY)] + [whole()] * 7 + [whole(pl.ANY)] * 2,
        out_specs=(whole(),) * 6 + (whole(pltpu.SMEM),) * 2,
        scratch_shapes=[
            pltpu.VMEM((blocks, cells, bins), F32),
            pltpu.VMEM((2 * bins, bins), F32),
            pltpu.VMEM((SEGMENT, 2 * bins), F32),
            pltpu.SMEM((1, 128), I32),
            pltpu.SMEM((1024,), I32),
            pltpu.SMEM((wide_count,), I32),
            pltpu.SemaphoreType.DMA((blocks // 8,)),
            pltpu.SemaphoreType.DMA((2,)),
        ],
        cost_estimate=cost(800000000, 4000000),
        compiler_params=pltpu.CompilerParams(vmem_limit_bytes=67043328),
    )(haze_bin_mass, wind_speed.T, vapour_t, *rates, targets.T, upwind_blocks)

    def fill_in(*refs):
        inflow_kernel(*refs, rank=coag_left.shape[1])

    packed = pl.pallas_call(
        fill_in,
        out_shape=packed_type,
        in_specs=[whole(pl.ANY)] + [whole()] * 8 + [whole(pltpu.SMEM)] * 2,
        out_specs=whole(pl.ANY),
        scratch_shapes=[
            pltpu.VMEM((3 * blocks, 2 * bins), F32),
            pltpu.VMEM((blocks, bins), F32),
            pltpu.VMEM((blocks, 2 * bins), F32),
            pltpu.SemaphoreType.DMA,
        ],
        input_output_aliases={0: 0},
        cost_estimate=cost(100000, 300000),
    )(packed, top, wind_top, same, low, high, first_both, first_low, second, slot, source)
    lines = wide_count // COLUMNS
    order = [line * COLUMNS + column for column in range(COLUMNS) for line in range(lines)]
    arrived = lax.all_to_all(
        packed, "wide", split_axis=0, concat_axis=0, tiled=True, axis_index_groups=[order]
    )
    arrived = arrived.reshape(COLUMNS, lines, 2, cells, bins)
    haze_output_slots = jnp.swapaxes(arrived, 0, 1).reshape(slots, cells, bins)
    vapour_out = pl.pallas_call(
        vapour_kernel,
        out_shape=shape(cells, blocks),
        in_specs=[whole()] * 3,
        out_specs=whole(),
        cost_estimate=cost(400000000, 1000000),
    )(haze_bin_mass, vapour_t, uptake_row)
    return (haze_output_slots, vapour_out.T)


def solution(mesh):
    in_specs = (
        P("wide", "narrow", None),
        P("wide", "narrow"),
        P("wide", "narrow"),
        P(),
        P(),
        P(),
        P(),
        P(),
        P(),
        P(),
    )
    out_specs = (P("wide", "narrow", None), P("wide", "narrow"))
    return jax.shard_map(local, mesh=mesh, in_specs=in_specs, out_specs=out_specs, check_vma=False)
```

time: 99.2 us -> 99.9 us (level)
  the two profiles are of different devices: /device:TPU:27 before, /device:TPU:99 now
where the time goes in v2:
time: 99.9 us; the launch traced here: 99.5 us
  waiting for transfers between devices  59.4 us (59%)
  starting transfers between devices  23.9 us (24%)
  Pallas kernels  11.6 us (12%)
  local copies, waits for them, and re-layouts  3.25 us (3%)
    all_to_all x1, waiting for transfers between devices, local(): lax.all_to_all(packed, 'wide', split_axis=0, concat_axis=0, tiled=True, a...  59.4 us
    all_to_all x1, starting transfers between devices, local(): lax.all_to_all(packed, 'wide', split_axis=0, concat_axis=0, tiled=True, a...  16 us
    ppermute x3, starting transfers between devices, passed(): return lax.ppermute(rim, ('wide', 'narrow'), route)  7.96 us
    pallas_call x1, Pallas kernels, local(): pl.pallas_call(pack_kernel, out_shape=(packed_type, shape(blocks, bins),...  6.54 us
    pallas_call x1, Pallas kernels, local(): pl.pallas_call(vapour_kernel, out_shape=shape(cells, blocks), in_specs=[w...  2.86 us
    pallas_call x1, Pallas kernels, local(): pl.pallas_call(fill_in, out_shape=packed_type, in_specs=[whole(pl.ANY)] +...  2.21 us
  transfers between devices with their start and end apart: 4, of which 1 were waited for; matrix products, arithmetic and copies ran while one was open for 0% of the time, Pallas kernels for 9%

profile of v2, /device:TPU:99, one launch (start us, length us, event | category | flops | bytes accessed | tf_op | source)
XLA Modules:
  0.0 99.5 jit_solution(5202677350598517291)
XLA Ops:
  0.6 0.7 slice_bitcast_fusion
  1.3 1.0 slice.6
  2.3 0.1 broadcast_in_dim.12
  2.4 0.6 pad_maximum_fusion
  3.0 1.8 %collective-permute-start = (f32[64,256]{1,0:T(8,128)}, f32[64,256]{1,0:T(8,128)}, u32[]{:S(2)}, u32[]{:S(2)}) collective-permute-start(f32[64,256]{1,0:T(8,128)} %pad_maximum_fusion), channel_id=1, source_target_pairs={{0,1},{1,2},{2,3},{3,4},{4,5},{5,6},{6,7},{7,0},{8,9},{9,10},{10,1... | collective-permute-start | bytes 196616 | tf_op jit(solution)/shard_map/ppermute | solution.py:270
  4.8 3.7 %collective-permute-start.1 = (f32[64,256]{1,0:T(8,128)}, f32[64,256]{1,0:T(8,128)}, u32[]{:S(2)}, u32[]{:S(2)}) collective-permute-start(f32[64,256]{1,0:T(8,128)} %pad_maximum_fusion), channel_id=1, source_target_pairs={{0,9},{1,10},{2,11},{3,12},{4,13},{5,14},{6,15},{7,8},{8,17},{9,18... | collective-permute-start | bytes 196616 | tf_op jit(solution)/shard_map/ppermute | solution.py:270
  8.5 2.5 %collective-permute-start.2 = (f32[64,256]{1,0:T(8,128)}, f32[64,256]{1,0:T(8,128)}, u32[]{:S(2)}, u32[]{:S(2)}) collective-permute-start(f32[64,256]{1,0:T(8,128)} %pad_maximum_fusion), channel_id=1, source_target_pairs={{0,505},{1,506},{2,507},{3,508},{4,509},{5,510},{6,511},{7,504},{8... | collective-permute-start | bytes 196616 | tf_op jit(solution)/shard_map/ppermute | solution.py:270
  11.0 6.5 %shard_map.113 = (f32[128,32,128]{2,1,0:T(8,128)}, f32[64,128]{1,0:T(8,128)}, f32[64,128]{1,0:T(8,128)}, bf16[256,256]{1,0:T(8,128)(2,1)}, bf16[128,256]{1,0:T(8...) custom-call(f32[64,32,128]{2,1,0:T(8,128)} %haze_ref.1, f32[32,64]{1,0:T(8,128)} %bitcast.19, ...), custom_call_target="tpu_custom_call" | custom-call | flops 800000000 | bytes 4000000 | tf_op jit(solution)/shard_map/pallas_call | solution.py:278
  17.5 0.0 collective-permute-done.refs_3_
  17.5 0.0 collective-permute-done.1.refs_4_
  17.6 0.0 collective-permute-done.2.refs_5_
  17.6 2.2 %shard_map.114 = f32[128,32,128]{2,1,0:T(8,128)} custom-call(f32[128,32,128]{2,1,0:T(8,128)} %get-tuple-element.10.refs_0_, f32[64,128]{1,0:T(8,128)} %get-tuple-element.11.refs_1_, f32[64,128]{1,0:T(8,128)} %get-tuple-element.12.refs_2_, f32[64,256]{1,0:T(8,128)} %collective-permute-done.refs_3_, ...), custom_call_target="tpu_custom_call", output_to_operand_aliasing={{}: (0, {})} | custom-call | flops 100000 | bytes 300000 | tf_op jit(solution)/shard_map/pallas_call | solution.py:309
  19.8 16.0 %all-to-all-start = ((f32[128,32,128]{2,1,0:T(8,128)}), f32[128,32,128]{2,1,0:T(8,128)S(1)}, u32[]{:S(2)}, u32[]{:S(2)}) async-start(f32[128,32,128]{2,1,0:T(8,128)} %shard_map.114), calls=%async_computation | async-start | bytes 4194304 | tf_op jit(solution)/shard_map/all_to_all | solution.py:325
  35.8 2.9 %shard_map.115 = f32[32,64]{1,0:T(8,128)} custom-call(f32[64,32,128]{2,1,0:T(8,128)} %haze_ref.1, f32[32,64]{1,0:T(8,128)} %bitcast.22, f32[1,128]{1,0:T(1,128)} %bitcast.26), custom_call_target="tpu_custom_call" | custom-call | flops 400000000 | bytes 1000000 | tf_op jit(solution)/shard_map/pallas_call | solution.py:330
  38.6 59.4 %all-to-all-done = f32[128,32,128]{2,1,0:T(8,128)S(1)} async-done(((f32[128,32,128]{2,1,0:T(8,128)}), f32[128,32,128]{2,1,0:T(8,128)S(1)}, u32[]{:S(2)}, u32[]{:S(2)}) %all-to-all-start) | async-done | bytes 2097184 | tf_op jit(solution)/shard_map/all_to_all | solution.py:325
  98.0 1.5 %copy.14 = f32[8,8,2,32,128]{4,3,2,1,0:T(8,128)} copy(f32[8,8,2,32,128]{4,3,2,0,1:T(8,128)S(1)} %bitcast.16) | data formatting | bytes 4194304 | tf_op jit(solution)/shard_map/transpose | solution.py:329
Async XLA Ops:
  3.0 14.5 %collective-permute-start = (f32[64,256]{1,0:T(8,128)}, f32[64,256]{1,0:T(8,128)}, u32[]{:S(2)}, u32[]{:S(2)}) collective-permute-start(f32[64,256]{1,0:T(8,128)} %pad_maximum_fusion), channel_id=1, source_target_pairs={{0,1},{1,2},{2,3},{3,4},{4,5},{5,6},{6,7},{7,0},{8,9},{9,10},{10,1... | collective-permute-start | bytes 196616 | tf_op jit(solution)/shard_map/ppermute | solution.py:270
  4.8 12.8 %collective-permute-start.1 = (f32[64,256]{1,0:T(8,128)}, f32[64,256]{1,0:T(8,128)}, u32[]{:S(2)}, u32[]{:S(2)}) collective-permute-start(f32[64,256]{1,0:T(8,128)} %pad_maximum_fusion), channel_id=1, source_target_pairs={{0,9},{1,10},{2,11},{3,12},{4,13},{5,14},{6,15},{7,8},{8,17},{9,18... | collective-permute-start | bytes 196616 | tf_op jit(solution)/shard_map/ppermute | solution.py:270
  8.5 9.1 %collective-permute-start.2 = (f32[64,256]{1,0:T(8,128)}, f32[64,256]{1,0:T(8,128)}, u32[]{:S(2)}, u32[]{:S(2)}) collective-permute-start(f32[64,256]{1,0:T(8,128)} %pad_maximum_fusion), channel_id=1, source_target_pairs={{0,505},{1,506},{2,507},{3,508},{4,509},{5,510},{6,511},{7,504},{8... | collective-permute-start | bytes 196616 | tf_op jit(solution)/shard_map/ppermute | solution.py:270
  19.8 78.2 %all-to-all-start = ((f32[128,32,128]{2,1,0:T(8,128)}), f32[128,32,128]{2,1,0:T(8,128)S(1)}, u32[]{:S(2)}, u32[]{:S(2)}) async-start(f32[128,32,128]{2,1,0:T(8,128)} %shard_map.114), calls=%async_computation | async-start | bytes 4194304 | tf_op jit(solution)/shard_map/all_to_all | solution.py:325

commit v3 on v2

--- a/solution.py
+++ b/solution.py
@@ -79,6 +79,45 @@
     return x + (rate[:, :bins] - x * rate[:, bins:])
 
 
+def rim_kernel(
+    haze_hbm,
+    vapour_ref,
+    uptake_ref,
+    left_ref,
+    right_ref,
+    gain_ref,
+    loss_ref,
+    rim_ref,
+    rows_buf,
+    columns,
+    second_buf,
+    first_both,
+    first_low,
+    second,
+    sem,
+):
+    cells = haze_hbm.shape[1]
+    copy = pltpu.make_async_copy(haze_hbm.at[:, cells - 1, :], rows_buf, sem)
+    copy.start()
+    fill_weights(
+        columns,
+        second_buf,
+        first_both,
+        first_low,
+        second,
+        left_ref[...],
+        right_ref[...],
+        uptake_ref[...],
+        gain_ref[...],
+        loss_ref[...],
+    )
+    vapour_rows = rows_of_lanes(vapour_ref[cells - 1 : cells, :], rows_buf.shape[1])
+    copy.wait()
+    rim_ref[...] = grow(
+        rows_buf[...], vapour_rows, first_both, first_low, second, left_ref.shape[0]
+    )
+
+
 def pack_kernel(
     haze_hbm,
     wind_ref,
@@ -93,14 +132,14 @@
     packed_ref,
     top_ref,
     wind_top_ref,
-    first_both,
-    first_low,
-    second,
     slot_ref,
     source_ref,
     haze_buf,
     columns,
     second_buf,
+    first_both,
+    first_low,
+    second,
     window,
     upwind_window,
     used,
@@ -150,13 +189,12 @@
     wind = wind_ref[...]
     vapour = vapour_ref[...]
     wind_top_ref[...] = rows_of_lanes(wind_ref[0:1, :], bins)
-    for copy in window_copies:
+    for copy in window_copies + copies:
         copy.wait()
     block_bits = blocks.bit_length() - 1
     column_bits = COLUMNS.bit_length() - 1
     line_bits = (wide_count // COLUMNS).bit_length() - 1
     for g in range(blocks // group):
-        copies[g].wait()
         x = haze_buf[g * group : (g + 1) * group].reshape(rows, bins)
         ids = range(g * group, (g + 1) * group)
         vapour_rows = jnp.concatenate([column_rows(vapour, b, cells, bins) for b in ids], 0)
@@ -187,27 +225,20 @@
     same_ref,
     low_ref,
     high_ref,
-    first_both,
-    first_low,
-    second,
     slot_ref,
     source_ref,
     packed_hbm,
     near,
     inflow,
-    rows_buf,
     sem,
-    *,
-    rank,
 ):
     blocks, bins = top_ref.shape
     near[0:blocks, :] = low_ref[...]
     near[blocks : 2 * blocks, :] = same_ref[...]
     near[2 * blocks :, :] = high_ref[...]
     for b in range(blocks):
-        rows_buf[b : b + 1, :] = near[pl.ds(source_ref[b], 1), :]
-    grown = grow(rows_buf[:, :bins], rows_buf[:, bins:], first_both, first_low, second, rank)
-    inflow[...] = top_ref[...] + wind_top_ref[...] * grown
+        inflow[b : b + 1, :] = near[pl.ds(source_ref[b], 1), :]
+    inflow[...] = top_ref[...] + wind_top_ref[...] * inflow[...]
     for b in range(blocks):
         pltpu.make_async_copy(inflow.at[b], packed_hbm.at[slot_ref[b], 0], sem).start()
     pltpu.make_async_copy(inflow, packed_hbm.at[pl.ds(0, blocks), 0, :], sem).wait()
@@ -254,45 +285,54 @@
     vapour_t = vapour.T
     uptake_row = uptake_rates[None, :]
     rates = (uptake_row, coag_left.T, coag_right.T, coag_gain, coag_loss)
-    rim = jnp.concatenate(
-        [haze_bin_mass[:, cells - 1, :], jnp.broadcast_to(vapour[:, cells - 1 :], (blocks, bins))], 1
-    )
-
-    def passed(distance):
-        route = [
-            (
-                w * narrow_count + n,
-                ((w + distance) % wide_count) * narrow_count + (n + 1) % narrow_count,
-            )
-            for w in range(wide_count)
-            for n in range(narrow_count)
-        ]
-        return lax.ppermute(rim, ("wide", "narrow"), route)
-
-    same, low, high = passed(0), passed(1), passed(-1)
-
     def shape(*dims, kind=F32):
         return jax.ShapeDtypeStruct(dims, kind)
 
+    weight_scratch = [
+        pltpu.VMEM((2 * bins, bins), F32),
+        pltpu.VMEM((SEGMENT, 2 * bins), F32),
+        pltpu.VMEM((2 * bins, 2 * bins), BF16),
+        pltpu.VMEM((bins, 2 * bins), BF16),
+        pltpu.VMEM((bins, 2 * bins), BF16),
+    ]
+    rows_type = shape(blocks, bins)
+    rim = pl.pallas_call(
+        rim_kernel,
+        out_shape=rows_type,
+        in_specs=[whole(pl.ANY)] + [whole()] * 6,
+        out_specs=whole(),
+        scratch_shapes=[
+            pltpu.VMEM((blocks, bins), F32),
+            *weight_scratch,
+            pltpu.SemaphoreType.DMA,
+        ],
+        cost_estimate=cost(10000000, 100000),
+    )(haze_bin_mass, vapour_t, *rates)
+    last = narrow_count - 1
+
+    def flat(w, n):
+        return (w % wide_count) * narrow_count + n % narrow_count
+
+    def passed(distance):
+        if distance == 0:
+            route = [
+                (flat(w, n), flat(w, n + 1)) for w in range(wide_count) for n in range(narrow_count)
+            ]
+        else:
+            route = [(flat(w, last), flat(w + distance, 0)) for w in range(wide_count)]
+            route += [(flat(w, n), flat(w, n)) for w in range(wide_count) for n in range(1, last)]
+        return lax.ppermute(rim, ("wide", "narrow"), route)
+
+    same, low, high = passed(0), passed(1), passed(-1)
     packed_type = shape(slots, cells, bins)
-    packed, top, wind_top, first_both, first_low, second, slot, source = pl.pallas_call(
+    packed, top, wind_top, slot, source = pl.pallas_call(
         pack_kernel,
-        out_shape=(
-            packed_type,
-            shape(blocks, bins),
-            shape(blocks, bins),
-            shape(2 * bins, 2 * bins, kind=BF16),
-            shape(bins, 2 * bins, kind=BF16),
-            shape(bins, 2 * bins, kind=BF16),
-            shape(blocks, kind=I32),
-            shape(blocks, kind=I32),
-        ),
+        out_shape=(packed_type, rows_type, rows_type, shape(blocks, kind=I32), shape(blocks, kind=I32)),
         in_specs=[whole(pl.ANY)] + [whole()] * 7 + [whole(pl.ANY)] * 2,
-        out_specs=(whole(),) * 6 + (whole(pltpu.SMEM),) * 2,
+        out_specs=(whole(),) * 3 + (whole(pltpu.SMEM),) * 2,
         scratch_shapes=[
             pltpu.VMEM((blocks, cells, bins), F32),
-            pltpu.VMEM((2 * bins, bins), F32),
-            pltpu.VMEM((SEGMENT, 2 * bins), F32),
+            *weight_scratch,
             pltpu.SMEM((1, 128), I32),
             pltpu.SMEM((1024,), I32),
             pltpu.SMEM((wide_count,), I32),
@@ -302,24 +342,19 @@
         cost_estimate=cost(800000000, 4000000),
         compiler_params=pltpu.CompilerParams(vmem_limit_bytes=67043328),
     )(haze_bin_mass, wind_speed.T, vapour_t, *rates, targets.T, upwind_blocks)
-
-    def fill_in(*refs):
-        inflow_kernel(*refs, rank=coag_left.shape[1])
-
     packed = pl.pallas_call(
-        fill_in,
+        inflow_kernel,
         out_shape=packed_type,
-        in_specs=[whole(pl.ANY)] + [whole()] * 8 + [whole(pltpu.SMEM)] * 2,
+        in_specs=[whole(pl.ANY)] + [whole()] * 5 + [whole(pltpu.SMEM)] * 2,
         out_specs=whole(pl.ANY),
         scratch_shapes=[
-            pltpu.VMEM((3 * blocks, 2 * bins), F32),
+            pltpu.VMEM((3 * blocks, bins), F32),
             pltpu.VMEM((blocks, bins), F32),
-            pltpu.VMEM((blocks, 2 * bins), F32),
             pltpu.SemaphoreType.DMA,
         ],
         input_output_aliases={0: 0},
         cost_estimate=cost(100000, 300000),
-    )(packed, top, wind_top, same, low, high, first_both, first_low, second, slot, source)
+    )(packed, top, wind_top, same, low, high, slot, source)
     lines = wide_count // COLUMNS
     order = [line * COLUMNS + column for column in range(COLUMNS) for line in range(lines)]
     arrived = lax.all_to_all(

time: 99.9 us -> 94.9 us (0.950)
  the two profiles are of different devices: /device:TPU:99 before, /device:TPU:119 now
where the time goes in v3:
time: 94.9 us; the launch traced here: 94.3 us
  waiting for transfers between devices  58.6 us (62%)
  starting transfers between devices  20.6 us (22%)
  Pallas kernels  12.8 us (13%)
  local copies, waits for them, and re-layouts  1.51 us (2%)
    all_to_all x1, waiting for transfers between devices, local(): lax.all_to_all(packed, 'wide', split_axis=0, concat_axis=0, tiled=True, a...  58.6 us
    all_to_all x1, starting transfers between devices, local(): lax.all_to_all(packed, 'wide', split_axis=0, concat_axis=0, tiled=True, a...  13.7 us
    ppermute x3, starting transfers between devices, passed(): return lax.ppermute(rim, ('wide', 'narrow'), route)  6.98 us
    pallas_call x1, Pallas kernels, local(): pl.pallas_call(pack_kernel, out_shape=(packed_type, rows_type, rows_type,...  5.82 us
    pallas_call x1, Pallas kernels, local(): pl.pallas_call(vapour_kernel, out_shape=shape(cells, blocks), in_specs=[w...  2.86 us
    pallas_call x1, Pallas kernels, local(): pl.pallas_call(rim_kernel, out_shape=rows_type, in_specs=[whole(pl.ANY)]...  2.47 us
  transfers between devices with their start and end apart: 4, of which 1 were waited for; matrix products, arithmetic and copies ran while one was open for 0% of the time, Pallas kernels for 9%

profile of v3, /device:TPU:119, one launch (start us, length us, event | category | flops | bytes accessed | tf_op | source)
XLA Modules:
  0.0 94.3 jit_solution(2538518715279308582)
XLA Ops:
  0.6 2.5 %shard_map.114 = f32[64,128]{1,0:T(8,128)} custom-call(f32[64,32,128]{2,1,0:T(8,128)} %haze_ref.1, f32[32,64]{1,0:T(8,128)} %bitcast.13, f32[1,128]{1,0:T(1,128)} %bitcast.20, f32[8,128]{1,0:T(8,128)} %bitcast.16, f32[8,128]{1,0:T(8,128)} %bitcast.18, f32[8,128]{1,0:T(8,128)} %gain_ref.3, f32[8,128]{1,0:T(8,128)} %loss_ref.3), custom_call_target="tpu_custom_call" | custom-call | flops 10000000 | bytes 100000 | tf_op jit(solution)/shard_map/pallas_call | solution.py:299
  3.1 0.8 collective-permute-start
  3.9 4.3 %collective-permute-start.1 = (f32[64,128]{1,0:T(8,128)}, f32[64,128]{1,0:T(8,128)}, u32[]{:S(2)}, u32[]{:S(2)}) collective-permute-start(f32[64,128]{1,0:T(8,128)} %shard_map.114), channel_id=1, source_target_pairs={{7,8},{15,16},{23,24},{31,32},{39,40},{47,48},{55,56},{63,64},{71,... | collective-permute-start | bytes 98312 | tf_op jit(solution)/shard_map/ppermute | solution.py:324
  8.2 1.9 %collective-permute-start.2 = (f32[64,128]{1,0:T(8,128)}, f32[64,128]{1,0:T(8,128)}, u32[]{:S(2)}, u32[]{:S(2)}) collective-permute-start(f32[64,128]{1,0:T(8,128)} %shard_map.114), channel_id=1, source_target_pairs={{7,504},{15,0},{23,8},{31,16},{39,24},{47,32},{55,40},{63,48},{71,... | collective-permute-start | bytes 98312 | tf_op jit(solution)/shard_map/ppermute | solution.py:324
  10.1 5.8 %shard_map.113 = (f32[128,32,128]{2,1,0:T(8,128)}, f32[64,128]{1,0:T(8,128)}, f32[64,128]{1,0:T(8,128)}, s32[64]{0:T(128)}, s32[64]{0:T(128)}) custom-call(f32[64,32,128]{2,1,0:T(8,128)} %haze_ref.1, f32[32,64]{1,0:T(8,128)} %bitcast.23, f32[32,64]{1,0:T(8,128)} %bitcast.14, f32[1,128]{1,0:T(1,128)} %bitcast.21, f32[8,128]{1,0:T(8,128)} %bitcast.17, ...), custom_call_target="tpu_custom_call" | custom-call | flops 800000000 | bytes 4000000 | tf_op jit(solution)/shard_map/pallas_call | solution.py:328
  15.9 0.0 collective-permute-done.same_ref
  15.9 0.0 collective-permute-done.1.low_ref
  15.9 0.0 collective-permute-done.2.high_ref
  15.9 1.7 %shard_map.115 = f32[128,32,128]{2,1,0:T(8,128)} custom-call(f32[128,32,128]{2,1,0:T(8,128)} %get-tuple-element.7.packed_in, f32[64,128]{1,0:T(8,128)} %get-tuple-element.8.top_ref, f32[64,128]{1,0:T(8,128)} %get-tuple-element.9.wind_top_ref, f32[64,128]{1,0:T(8,128)} %collective-permute-done.same_ref, ...), custom_call_target="tpu_custom_call", output_to_operand_aliasing={{}: (0, {})} | custom-call | flops 100000 | bytes 300000 | tf_op jit(solution)/shard_map/pallas_call | solution.py:345
  17.6 13.7 %all-to-all-start = ((f32[128,32,128]{2,1,0:T(8,128)}), f32[128,32,128]{2,1,0:T(8,128)S(1)}, u32[]{:S(2)}, u32[]{:S(2)}) async-start(f32[128,32,128]{2,1,0:T(8,128)} %shard_map.115), calls=%async_computation | async-start | bytes 4194304 | tf_op jit(solution)/shard_map/all_to_all | solution.py:360
  31.3 2.9 %shard_map.116 = f32[32,64]{1,0:T(8,128)} custom-call(f32[64,32,128]{2,1,0:T(8,128)} %haze_ref.1, f32[32,64]{1,0:T(8,128)} %bitcast.15, f32[1,128]{1,0:T(1,128)} %bitcast.22), custom_call_target="tpu_custom_call" | custom-call | flops 400000000 | bytes 1000000 | tf_op jit(solution)/shard_map/pallas_call | solution.py:365
  34.1 58.6 %all-to-all-done = f32[128,32,128]{2,1,0:T(8,128)S(1)} async-done(((f32[128,32,128]{2,1,0:T(8,128)}), f32[128,32,128]{2,1,0:T(8,128)S(1)}, u32[]{:S(2)}, u32[]{:S(2)}) %all-to-all-start) | async-done | bytes 2097184 | tf_op jit(solution)/shard_map/all_to_all | solution.py:360
  92.8 1.5 %copy.13 = f32[8,8,2,32,128]{4,3,2,1,0:T(8,128)} copy(f32[8,8,2,32,128]{4,3,2,0,1:T(8,128)S(1)} %bitcast.11) | data formatting | bytes 4194304 | tf_op jit(solution)/shard_map/transpose | solution.py:364
Async XLA Ops:
  3.1 12.8 %collective-permute-start = (f32[64,128]{1,0:T(8,128)}, f32[64,128]{1,0:T(8,128)}, u32[]{:S(2)}, u32[]{:S(2)}) collective-permute-start(f32[64,128]{1,0:T(8,128)} %shard_map.114), channel_id=1, source_target_pairs={{0,1},{1,2},{2,3},{3,4},{4,5},{5,6},{6,7},{7,0},{8,9},{9,10},{10,1... | collective-permute-start | bytes 98312 | tf_op jit(solution)/shard_map/ppermute | solution.py:324
  3.9 12.1 %collective-permute-start.1 = (f32[64,128]{1,0:T(8,128)}, f32[64,128]{1,0:T(8,128)}, u32[]{:S(2)}, u32[]{:S(2)}) collective-permute-start(f32[64,128]{1,0:T(8,128)} %shard_map.114), channel_id=1, source_target_pairs={{7,8},{15,16},{23,24},{31,32},{39,40},{47,48},{55,56},{63,64},{71,... | collective-permute-start | bytes 98312 | tf_op jit(solution)/shard_map/ppermute | solution.py:324
  8.2 7.7 %collective-permute-start.2 = (f32[64,128]{1,0:T(8,128)}, f32[64,128]{1,0:T(8,128)}, u32[]{:S(2)}, u32[]{:S(2)}) collective-permute-start(f32[64,128]{1,0:T(8,128)} %shard_map.114), channel_id=1, source_target_pairs={{7,504},{15,0},{23,8},{31,16},{39,24},{47,32},{55,40},{63,48},{71,... | collective-permute-start | bytes 98312 | tf_op jit(solution)/shard_map/ppermute | solution.py:324
  17.6 75.1 %all-to-all-start = ((f32[128,32,128]{2,1,0:T(8,128)}), f32[128,32,128]{2,1,0:T(8,128)S(1)}, u32[]{:S(2)}, u32[]{:S(2)}) async-start(f32[128,32,128]{2,1,0:T(8,128)} %shard_map.115), calls=%async_computation | async-start | bytes 4194304 | tf_op jit(solution)/shard_map/all_to_all | solution.py:360

commit v4 on v3

--- a/solution.py
+++ b/solution.py
@@ -127,8 +127,8 @@
     right_ref,
     gain_ref,
     loss_ref,
+    upwind_ref,
     targets_hbm,
-    upwind_hbm,
     packed_ref,
     top_ref,
     wind_top_ref,
@@ -141,29 +141,23 @@
     first_low,
     second,
     window,
-    upwind_window,
     used,
     haze_sems,
-    window_sems,
+    window_sem,
 ):
     blocks, cells, bins = haze_buf.shape
     rank = left_ref.shape[0]
-    group = 8
+    group = 64
     rows = group * cells
     wide_count = lax.axis_size("wide")
     owner = lax.axis_index("wide")
     first = lax.axis_index("narrow") == 0
     start = owner * blocks
     base = pl.multiple_of((start // 128) * 128, 128)
-    far_base = pl.multiple_of((start // 1024) * 1024, 1024)
-    window_copies = [
-        pltpu.make_async_copy(targets_hbm.at[:, pl.ds(base, 128)], window, window_sems.at[0]),
-        pltpu.make_async_copy(
-            upwind_hbm.at[pl.ds(far_base, 1024)], upwind_window, window_sems.at[1]
-        ),
-    ]
-    for copy in window_copies:
-        copy.start()
+    window_copy = pltpu.make_async_copy(
+        targets_hbm.at[:, pl.ds(base, 128)], window, window_sem
+    )
+    window_copy.start()
     copies = []
     for g in range(blocks // group):
         part = pl.ds(g * group, group)
@@ -171,8 +165,10 @@
         copy.start()
         copies.append(copy)
     packed_ref[...] = jnp.zeros_like(packed_ref)
-    for t in range(used.shape[0]):
-        used[t] = 0
+    lines = wide_count // COLUMNS
+    odd = lax.axis_index("narrow") & 1
+    for t in range(wide_count):
+        used[t] = jnp.where(odd == 1, 2 * t, 2 * ((t % COLUMNS) * lines + t // COLUMNS))
     fill_weights(
         columns,
         second_buf,
@@ -189,11 +185,14 @@
     wind = wind_ref[...]
     vapour = vapour_ref[...]
     wind_top_ref[...] = rows_of_lanes(wind_ref[0:1, :], bins)
-    for copy in window_copies + copies:
+    upwind = upwind_ref[pl.ds(start // 128, 1), :]
+    block_bits = blocks.bit_length() - 1
+    relative = ((upwind >> block_bits) - owner + 1 + wide_count) & (wide_count - 1)
+    far = (relative << block_bits) + (upwind & (blocks - 1))
+    near = blocks + (lax.broadcasted_iota(I32, far.shape, 1) & (blocks - 1))
+    source_ref[...] = jnp.where(first, far, near)
+    for copy in [window_copy] + copies:
         copy.wait()
-    block_bits = blocks.bit_length() - 1
-    column_bits = COLUMNS.bit_length() - 1
-    line_bits = (wide_count // COLUMNS).bit_length() - 1
     for g in range(blocks // group):
         x = haze_buf[g * group : (g + 1) * group].reshape(rows, bins)
         ids = range(g * group, (g + 1) * group)
@@ -205,17 +204,11 @@
         for j, b in enumerate(ids):
             at = j * cells
             target = window[0, start - base + b]
-            rank_within = used[target]
-            used[target] = rank_within + 1
-            position = ((target & (COLUMNS - 1)) << line_bits) + (target >> column_bits)
-            slot = position * 2 + rank_within
+            slot = used[target]
+            used[target] = slot + 1
             slot_ref[b] = slot
             packed_ref[slot] = moved[at : at + cells, :]
             top_ref[b : b + 1, :] = moved[at : at + 1, :]
-            source = upwind_window[start - far_base + b]
-            relative = ((source >> block_bits) - owner + 1 + wide_count) & (wide_count - 1)
-            far = (relative << block_bits) + (source & (blocks - 1))
-            source_ref[b] = jnp.where(first, far, blocks + b)
 
 
 def inflow_kernel(
@@ -236,12 +229,25 @@
     near[0:blocks, :] = low_ref[...]
     near[blocks : 2 * blocks, :] = same_ref[...]
     near[2 * blocks :, :] = high_ref[...]
+    offset = (lax.axis_index("wide") * blocks) % 128
     for b in range(blocks):
-        inflow[b : b + 1, :] = near[pl.ds(source_ref[b], 1), :]
+        inflow[b : b + 1, :] = near[pl.ds(source_ref[0, offset + b], 1), :]
     inflow[...] = top_ref[...] + wind_top_ref[...] * inflow[...]
     for b in range(blocks):
         pltpu.make_async_copy(inflow.at[b], packed_hbm.at[slot_ref[b], 0], sem).start()
     pltpu.make_async_copy(inflow, packed_hbm.at[pl.ds(0, blocks), 0, :], sem).wait()
+
+
+def place_kernel(arrived_ref, out_hbm, sem):
+    wide_count = lax.axis_size("wide")
+    lines = wide_count // COLUMNS
+    odd = lax.axis_index("narrow") & 1
+    for p in range(wide_count):
+        source = jnp.where(odd == 1, p, (p % lines) * COLUMNS + p // lines)
+        pltpu.make_async_copy(
+            arrived_ref.at[pl.ds(2 * p, 2)], out_hbm.at[pl.ds(2 * source, 2)], sem
+        ).start()
+    pltpu.make_async_copy(arrived_ref, out_hbm, sem).wait()
 
 
 def vapour_kernel(haze_ref, vapour_ref, uptake_ref, vapour_out_ref):
@@ -308,6 +314,7 @@
         ],
         cost_estimate=cost(10000000, 100000),
     )(haze_bin_mass, vapour_t, *rates)
+    both = ("wide", "narrow")
     last = narrow_count - 1
 
     def flat(w, n):
@@ -320,28 +327,26 @@
             ]
         else:
             route = [(flat(w, last), flat(w + distance, 0)) for w in range(wide_count)]
-            route += [(flat(w, n), flat(w, n)) for w in range(wide_count) for n in range(1, last)]
-        return lax.ppermute(rim, ("wide", "narrow"), route)
+        return lax.ppermute(rim, both, route)
 
     same, low, high = passed(0), passed(1), passed(-1)
     packed_type = shape(slots, cells, bins)
     packed, top, wind_top, slot, source = pl.pallas_call(
         pack_kernel,
-        out_shape=(packed_type, rows_type, rows_type, shape(blocks, kind=I32), shape(blocks, kind=I32)),
-        in_specs=[whole(pl.ANY)] + [whole()] * 7 + [whole(pl.ANY)] * 2,
-        out_specs=(whole(),) * 3 + (whole(pltpu.SMEM),) * 2,
+        out_shape=(packed_type, rows_type, rows_type, shape(blocks, kind=I32), shape(1, 128, kind=I32)),
+        in_specs=[whole(pl.ANY)] + [whole()] * 8 + [whole(pl.ANY)],
+        out_specs=(whole(),) * 3 + (whole(pltpu.SMEM), whole()),
         scratch_shapes=[
             pltpu.VMEM((blocks, cells, bins), F32),
             *weight_scratch,
             pltpu.SMEM((1, 128), I32),
-            pltpu.SMEM((1024,), I32),
             pltpu.SMEM((wide_count,), I32),
-            pltpu.SemaphoreType.DMA((blocks // 8,)),
-            pltpu.SemaphoreType.DMA((2,)),
+            pltpu.SemaphoreType.DMA((blocks // 64,)),
+            pltpu.SemaphoreType.DMA,
         ],
         cost_estimate=cost(800000000, 4000000),
         compiler_params=pltpu.CompilerParams(vmem_limit_bytes=67043328),
-    )(haze_bin_mass, wind_speed.T, vapour_t, *rates, targets.T, upwind_blocks)
+    )(haze_bin_mass, wind_speed.T, vapour_t, *rates, upwind_blocks.reshape(-1, 128), targets.T)
     packed = pl.pallas_call(
         inflow_kernel,
         out_shape=packed_type,
@@ -357,11 +362,22 @@
     )(packed, top, wind_top, same, low, high, slot, source)
     lines = wide_count // COLUMNS
     order = [line * COLUMNS + column for column in range(COLUMNS) for line in range(lines)]
+    groups = [
+        [w * narrow_count + n for w in (range(wide_count) if n % 2 else order)]
+        for n in range(narrow_count)
+    ]
     arrived = lax.all_to_all(
-        packed, "wide", split_axis=0, concat_axis=0, tiled=True, axis_index_groups=[order]
-    )
-    arrived = arrived.reshape(COLUMNS, lines, 2, cells, bins)
-    haze_output_slots = jnp.swapaxes(arrived, 0, 1).reshape(slots, cells, bins)
+        packed, both, split_axis=0, concat_axis=0, tiled=True, axis_index_groups=groups
+    )
+    haze_output_slots = pl.pallas_call(
+        place_kernel,
+        out_shape=packed_type,
+        in_specs=[whole(pl.ANY)],
+        out_specs=whole(pl.ANY),
+        scratch_shapes=[pltpu.SemaphoreType.DMA],
+        cost_estimate=cost(0, 4000000),
+        compiler_params=pltpu.CompilerParams(vmem_limit_bytes=1048576),
+    )(arrived)
     vapour_out = pl.pallas_call(
         vapour_kernel,
         out_shape=shape(cells, blocks),

time: 94.9 us -> 85.5 us (0.901)
  the two profiles are of different devices: /device:TPU:119 before, /device:TPU:34 now
where the time goes in v4:
time: 85.5 us; the launch traced here: 84.9 us
  waiting for transfers between devices  52.1 us (61%)
  starting transfers between devices  18.8 us (22%)
  Pallas kernels  13.4 us (16%)
    all_to_all x1, waiting for transfers between devices, local(): lax.all_to_all(packed, both, split_axis=0, concat_axis=0, tiled=True, axi...  52 us
    all_to_all x1, starting transfers between devices, local(): lax.all_to_all(packed, both, split_axis=0, concat_axis=0, tiled=True, axi...  16.3 us
    pallas_call x1, Pallas kernels, local(): pl.pallas_call(pack_kernel, out_shape=(packed_type, rows_type, rows_type,...  5.08 us
    pallas_call x1, Pallas kernels, local(): pl.pallas_call(vapour_kernel, out_shape=shape(cells, blocks), in_specs=[w...  2.86 us
    ppermute x3, starting transfers between devices, passed(): return lax.ppermute(rim, both, route)  2.53 us
    pallas_call x1, Pallas kernels, local(): pl.pallas_call(rim_kernel, out_shape=rows_type, in_specs=[whole(pl.ANY)]...  2.47 us
  transfers between devices with their start and end apart: 4, of which 1 were waited for; matrix products, arithmetic and copies ran while one was open for 0% of the time, Pallas kernels for 9%

profile of v4, /device:TPU:34, one launch (start us, length us, event | category | flops | bytes accessed | tf_op | source)
XLA Modules:
  0.0 84.9 jit_solution(18322513583547394723)
XLA Ops:
  0.6 2.5 %shard_map.114 = f32[64,128]{1,0:T(8,128)} custom-call(f32[64,32,128]{2,1,0:T(8,128)} %haze_ref.1, f32[32,64]{1,0:T(8,128)} %bitcast.8, f32[1,128]{1,0:T(1,128)} %bitcast.15, f32[8,128]{1,0:T(8,128)} %bitcast.11, f32[8,128]{1,0:T(8,128)} %bitcast.13, f32[8,128]{1,0:T(8,128)} %gain_ref.3, f32[8,128]{1,0:T(8,128)} %loss_ref.3), custom_call_target="tpu_custom_call" | custom-call | flops 10000000 | bytes 100000 | tf_op jit(solution)/shard_map/pallas_call | solution.py:305
  3.1 0.0 collective-permute-start
  3.1 1.3 %collective-permute-start.1 = (f32[64,128]{1,0:T(8,128)}, f32[64,128]{1,0:T(8,128)}, u32[]{:S(2)}, u32[]{:S(2)}) collective-permute-start(f32[64,128]{1,0:T(8,128)} %shard_map.114), channel_id=1, source_target_pairs={{7,8},{15,16},{23,24},{31,32},{39,40},{47,48},{55,56},{63,64},{71,... | collective-permute-start | bytes 98312 | tf_op jit(solution)/shard_map/ppermute | solution.py:330
  4.4 1.2 %collective-permute-start.2 = (f32[64,128]{1,0:T(8,128)}, f32[64,128]{1,0:T(8,128)}, u32[]{:S(2)}, u32[]{:S(2)}) collective-permute-start(f32[64,128]{1,0:T(8,128)} %shard_map.114), channel_id=1, source_target_pairs={{7,504},{15,0},{23,8},{31,16},{39,24},{47,32},{55,40},{63,48},{71,... | collective-permute-start | bytes 98312 | tf_op jit(solution)/shard_map/ppermute | solution.py:330
  5.6 5.1 %shard_map.113 = (f32[128,32,128]{2,1,0:T(8,128)}, f32[64,128]{1,0:T(8,128)}, f32[64,128]{1,0:T(8,128)}, s32[64]{0:T(128)}, s32[1,128]{1,0:T(1,128)}) custom-call(f32[64,32,128]{2,1,0:T(8,128)} %haze_ref.1, f32[32,64]{1,0:T(8,128)} %bitcast.18, f32[32,64]{1,0:T(8,128)} %bitcast.9, f32[1,128]{1,0:T(1,128)} %bitcast.16, f32[8,128]{1,0:T(8,128)} %bitcast.12, ...), custom_call_target="tpu_custom_call" | custom-call | flops 800000000 | bytes 4000000 | tf_op jit(solution)/shard_map/pallas_call | solution.py:334
  10.7 0.0 collective-permute-done.same_ref
  10.7 0.0 collective-permute-done.1.low_ref
  10.8 0.0 collective-permute-done.2.high_ref
  10.8 1.7 %shard_map.115 = f32[128,32,128]{2,1,0:T(8,128)} custom-call(f32[128,32,128]{2,1,0:T(8,128)} %get-tuple-element.7.packed_in, f32[64,128]{1,0:T(8,128)} %get-tuple-element.8.top_ref, f32[64,128]{1,0:T(8,128)} %get-tuple-element.9.wind_top_ref, f32[64,128]{1,0:T(8,128)} %collective-permute-done.same_ref, ...), custom_call_target="tpu_custom_call", output_to_operand_aliasing={{}: (0, {})} | custom-call | flops 100000 | bytes 300000 | tf_op jit(solution)/shard_map/pallas_call | solution.py:350
  12.5 16.3 %all-to-all-start = ((f32[128,32,128]{2,1,0:T(8,128)}), f32[128,32,128]{2,1,0:T(8,128)S(1)}, u32[]{:S(2)}, u32[]{:S(2)}) async-start(f32[128,32,128]{2,1,0:T(8,128)} %shard_map.115), calls=%async_computation | async-start | bytes 4194304 | tf_op jit(solution)/shard_map/all_to_all | solution.py:369
  28.7 2.9 %shard_map.117 = f32[32,64]{1,0:T(8,128)} custom-call(f32[64,32,128]{2,1,0:T(8,128)} %haze_ref.1, f32[32,64]{1,0:T(8,128)} %bitcast.10, f32[1,128]{1,0:T(1,128)} %bitcast.17), custom_call_target="tpu_custom_call" | custom-call | flops 400000000 | bytes 1000000 | tf_op jit(solution)/shard_map/pallas_call | solution.py:381
  31.6 52.0 %all-to-all-done.arrived_ref = f32[128,32,128]{2,1,0:T(8,128)S(1)} async-done(((f32[128,32,128]{2,1,0:T(8,128)}), f32[128,32,128]{2,1,0:T(8,128)S(1)}, u32[]{:S(2)}, u32[]{:S(2)}) %all-to-all-start) | async-done | bytes 2097184 | tf_op jit(solution)/shard_map/all_to_all | solution.py:369
  83.6 1.3 %shard_map.116 = f32[128,32,128]{2,1,0:T(8,128)} custom-call(f32[128,32,128]{2,1,0:T(8,128)S(1)} %all-to-all-done.arrived_ref), custom_call_target="tpu_custom_call" | custom-call | bytes 4000000 | tf_op jit(solution)/shard_map/pallas_call | solution.py:372
Async XLA Ops:
  3.1 7.6 %collective-permute-start = (f32[64,128]{1,0:T(8,128)}, f32[64,128]{1,0:T(8,128)}, u32[]{:S(2)}, u32[]{:S(2)}) collective-permute-start(f32[64,128]{1,0:T(8,128)} %shard_map.114), channel_id=1, source_target_pairs={{0,1},{1,2},{2,3},{3,4},{4,5},{5,6},{6,7},{7,0},{8,9},{9,10},{10,1... | collective-permute-start | bytes 98312 | tf_op jit(solution)/shard_map/ppermute | solution.py:330
  3.1 7.6 %collective-permute-start.1 = (f32[64,128]{1,0:T(8,128)}, f32[64,128]{1,0:T(8,128)}, u32[]{:S(2)}, u32[]{:S(2)}) collective-permute-start(f32[64,128]{1,0:T(8,128)} %shard_map.114), channel_id=1, source_target_pairs={{7,8},{15,16},{23,24},{31,32},{39,40},{47,48},{55,56},{63,64},{71,... | collective-permute-start | bytes 98312 | tf_op jit(solution)/shard_map/ppermute | solution.py:330
  4.4 6.4 %collective-permute-start.2 = (f32[64,128]{1,0:T(8,128)}, f32[64,128]{1,0:T(8,128)}, u32[]{:S(2)}, u32[]{:S(2)}) collective-permute-start(f32[64,128]{1,0:T(8,128)} %shard_map.114), channel_id=1, source_target_pairs={{7,504},{15,0},{23,8},{31,16},{39,24},{47,32},{55,40},{63,48},{71,... | collective-permute-start | bytes 98312 | tf_op jit(solution)/shard_map/ppermute | solution.py:330
  12.5 71.2 %all-to-all-start = ((f32[128,32,128]{2,1,0:T(8,128)}), f32[128,32,128]{2,1,0:T(8,128)S(1)}, u32[]{:S(2)}, u32[]{:S(2)}) async-start(f32[128,32,128]{2,1,0:T(8,128)} %shard_map.115), calls=%async_computation | async-start | bytes 4194304 | tf_op jit(solution)/shard_map/all_to_all | solution.py:369

commit v5 on v4

--- a/solution.py
+++ b/solution.py
@@ -79,26 +79,49 @@
     return x + (rate[:, :bins] - x * rate[:, bins:])
 
 
+def fetched(sources, targets, sems):
+    copies = []
+    for i, (source, target) in enumerate(zip(sources, targets, strict=True)):
+        copy = pltpu.make_async_copy(source, target, sems.at[i])
+        copy.start()
+        copies.append(copy)
+    return copies
+
+
 def rim_kernel(
     haze_hbm,
+    vapour_hbm,
+    uptake_hbm,
+    left_hbm,
+    right_hbm,
+    gain_hbm,
+    loss_hbm,
+    rim_ref,
+    rows_buf,
     vapour_ref,
     uptake_ref,
     left_ref,
     right_ref,
     gain_ref,
     loss_ref,
-    rim_ref,
-    rows_buf,
     columns,
     second_buf,
     first_both,
     first_low,
     second,
     sem,
+    small_sems,
 ):
     cells = haze_hbm.shape[1]
     copy = pltpu.make_async_copy(haze_hbm.at[:, cells - 1, :], rows_buf, sem)
     copy.start()
+    small = fetched(
+        (vapour_hbm, uptake_hbm, left_hbm, right_hbm, gain_hbm, loss_hbm),
+        (vapour_ref, uptake_ref, left_ref, right_ref, gain_ref, loss_ref),
+        small_sems,
+    )
+    for part in small:
+        part.wait()
     fill_weights(
         columns,
         second_buf,
@@ -120,6 +143,21 @@
 
 def pack_kernel(
     haze_hbm,
+    wind_hbm,
+    vapour_hbm,
+    uptake_hbm,
+    left_hbm,
+    right_hbm,
+    gain_hbm,
+    loss_hbm,
+    upwind_hbm,
+    targets_hbm,
+    packed_ref,
+    top_ref,
+    wind_top_ref,
+    slot_ref,
+    source_ref,
+    haze_buf,
     wind_ref,
     vapour_ref,
     uptake_ref,
@@ -128,13 +166,6 @@
     gain_ref,
     loss_ref,
     upwind_ref,
-    targets_hbm,
-    packed_ref,
-    top_ref,
-    wind_top_ref,
-    slot_ref,
-    source_ref,
-    haze_buf,
     columns,
     second_buf,
     first_both,
@@ -144,6 +175,7 @@
     used,
     haze_sems,
     window_sem,
+    small_sems,
 ):
     blocks, cells, bins = haze_buf.shape
     rank = left_ref.shape[0]
@@ -164,11 +196,18 @@
         copy = pltpu.make_async_copy(haze_hbm.at[part], haze_buf.at[part], haze_sems.at[g])
         copy.start()
         copies.append(copy)
+    small = fetched(
+        (wind_hbm, vapour_hbm, uptake_hbm, left_hbm, right_hbm, gain_hbm, loss_hbm, upwind_hbm),
+        (wind_ref, vapour_ref, uptake_ref, left_ref, right_ref, gain_ref, loss_ref, upwind_ref),
+        small_sems,
+    )
     packed_ref[...] = jnp.zeros_like(packed_ref)
     lines = wide_count // COLUMNS
     odd = lax.axis_index("narrow") & 1
     for t in range(wide_count):
         used[t] = jnp.where(odd == 1, 2 * t, 2 * ((t % COLUMNS) * lines + t // COLUMNS))
+    for part in small:
+        part.wait()
     fill_weights(
         columns,
         second_buf,
@@ -305,12 +344,15 @@
     rim = pl.pallas_call(
         rim_kernel,
         out_shape=rows_type,
-        in_specs=[whole(pl.ANY)] + [whole()] * 6,
+        in_specs=[whole(pl.ANY)] * 7,
         out_specs=whole(),
         scratch_shapes=[
             pltpu.VMEM((blocks, bins), F32),
+            pltpu.VMEM(vapour_t.shape, F32),
+            *[pltpu.VMEM(rate.shape, F32) for rate in rates],
             *weight_scratch,
             pltpu.SemaphoreType.DMA,
+            pltpu.SemaphoreType.DMA((6,)),
         ],
         cost_estimate=cost(10000000, 100000),
     )(haze_bin_mass, vapour_t, *rates)
@@ -331,22 +373,28 @@
 
     same, low, high = passed(0), passed(1), passed(-1)
     packed_type = shape(slots, cells, bins)
+    upwind_rows = upwind_blocks.reshape(-1, 128)
     packed, top, wind_top, slot, source = pl.pallas_call(
         pack_kernel,
         out_shape=(packed_type, rows_type, rows_type, shape(blocks, kind=I32), shape(1, 128, kind=I32)),
-        in_specs=[whole(pl.ANY)] + [whole()] * 8 + [whole(pl.ANY)],
+        in_specs=[whole(pl.ANY)] * 10,
         out_specs=(whole(),) * 3 + (whole(pltpu.SMEM), whole()),
         scratch_shapes=[
             pltpu.VMEM((blocks, cells, bins), F32),
+            pltpu.VMEM(vapour_t.shape, F32),
+            pltpu.VMEM(vapour_t.shape, F32),
+            *[pltpu.VMEM(rate.shape, F32) for rate in rates],
+            pltpu.VMEM(upwind_rows.shape, I32),
             *weight_scratch,
             pltpu.SMEM((1, 128), I32),
             pltpu.SMEM((wide_count,), I32),
             pltpu.SemaphoreType.DMA((blocks // 64,)),
             pltpu.SemaphoreType.DMA,
+            pltpu.SemaphoreType.DMA((8,)),
         ],
         cost_estimate=cost(800000000, 4000000),
         compiler_params=pltpu.CompilerParams(vmem_limit_bytes=67043328),
-    )(haze_bin_mass, wind_speed.T, vapour_t, *rates, upwind_blocks.reshape(-1, 128), targets.T)
+    )(haze_bin_mass, wind_speed.T, vapour_t, *rates, upwind_rows, targets.T)
     packed = pl.pallas_call(
         inflow_kernel,
         out_shape=packed_type,

time: 85.5 us -> 86.1 us (level)
  the two profiles are of different devices: /device:TPU:34 before, /device:TPU:24 now
where the time goes in v5:
time: 86.1 us; the launch traced here: 85.6 us
  waiting for transfers between devices  57.4 us (67%)
  starting transfers between devices  15.5 us (18%)
  Pallas kernels  12 us (14%)
    all_to_all x1, waiting for transfers between devices, local(): lax.all_to_all(packed, both, split_axis=0, concat_axis=0, tiled=True, axi...  49.7 us
    all_to_all x1, starting transfers between devices, local(): lax.all_to_all(packed, both, split_axis=0, concat_axis=0, tiled=True, axi...  12.9 us
    ppermute x3, waiting for transfers between devices, passed(): return lax.ppermute(rim, both, route)  7.67 us
    pallas_call x1, Pallas kernels, local(): pl.pallas_call(pack_kernel, out_shape=(packed_type, rows_type, rows_type,...  4.2 us
    pallas_call x1, Pallas kernels, local(): pl.pallas_call(vapour_kernel, out_shape=shape(cells, blocks), in_specs=[w...  2.87 us
    ppermute x3, starting transfers between devices, passed(): return lax.ppermute(rim, both, route)  2.6 us
    pallas_call x1, Pallas kernels, local(): pl.pallas_call(rim_kernel, out_shape=rows_type, in_specs=[whole(pl.ANY)]...  1.95 us
  transfers between devices with their start and end apart: 4, of which 2 were waited for; matrix products, arithmetic and copies ran while one was open for 0% of the time, Pallas kernels for 8%

profile of v5, /device:TPU:24, one launch (start us, length us, event | category | flops | bytes accessed | tf_op | source)
XLA Modules:
  0.0 85.6 jit_solution(12866867482011647365)
XLA Ops:
  0.6 1.9 %shard_map.114 = f32[64,128]{1,0:T(8,128)} custom-call(f32[64,32,128]{2,1,0:T(8,128)} %haze_ref.1, f32[32,64]{1,0:T(8,128)} %bitcast.8, f32[1,128]{1,0:T(1,128)} %bitcast.15, f32[8,128]{1,0:T(8,128)} %bitcast.11, f32[8,128]{1,0:T(8,128)} %bitcast.13, f32[8,128]{1,0:T(8,128)} %gain_hbm.3, f32[8,128]{1,0:T(8,128)} %loss_hbm.3), custom_call_target="tpu_custom_call" | custom-call | flops 10000000 | bytes 100000 | tf_op jit(solution)/shard_map/pallas_call | solution.py:344
  2.6 0.0 collective-permute-start
  2.6 1.3 %collective-permute-start.1 = (f32[64,128]{1,0:T(8,128)}, f32[64,128]{1,0:T(8,128)}, u32[]{:S(2)}, u32[]{:S(2)}) collective-permute-start(f32[64,128]{1,0:T(8,128)} %shard_map.114), channel_id=1, source_target_pairs={{7,8},{15,16},{23,24},{31,32},{39,40},{47,48},{55,56},{63,64},{71,... | collective-permute-start | bytes 98312 | tf_op jit(solution)/shard_map/ppermute | solution.py:372
  3.9 1.3 %collective-permute-start.2 = (f32[64,128]{1,0:T(8,128)}, f32[64,128]{1,0:T(8,128)}, u32[]{:S(2)}, u32[]{:S(2)}) collective-permute-start(f32[64,128]{1,0:T(8,128)} %shard_map.114), channel_id=1, source_target_pairs={{7,504},{15,0},{23,8},{31,16},{39,24},{47,32},{55,40},{63,48},{71,... | collective-permute-start | bytes 98312 | tf_op jit(solution)/shard_map/ppermute | solution.py:372
  5.2 4.2 %shard_map.113 = (f32[128,32,128]{2,1,0:T(8,128)}, f32[64,128]{1,0:T(8,128)}, f32[64,128]{1,0:T(8,128)}, s32[64]{0:T(128)}, s32[1,128]{1,0:T(1,128)}) custom-call(f32[64,32,128]{2,1,0:T(8,128)} %haze_ref.1, f32[32,64]{1,0:T(8,128)} %bitcast.18, f32[32,64]{1,0:T(8,128)} %bitcast.9, f32[1,128]{1,0:T(1,128)} %bitcast.16, f32[8,128]{1,0:T(8,128)} %bitcast.12, ...), custom_call_target="tpu_custom_call" | custom-call | flops 800000000 | bytes 4000000 | tf_op jit(solution)/shard_map/pallas_call | solution.py:377
  9.4 0.0 collective-permute-done.same_ref
  9.4 7.7 %collective-permute-done.1.low_ref = f32[64,128]{1,0:T(8,128)} collective-permute-done((f32[64,128]{1,0:T(8,128)}, f32[64,128]{1,0:T(8,128)}, u32[]{:S(2)}, u32[]{:S(2)}) %collective-permute-start.1) | collective-permute-done | bytes 32800 | tf_op jit(solution)/shard_map/ppermute | solution.py:372
  17.1 0.0 collective-permute-done.2.high_ref
  17.1 1.7 %shard_map.115 = f32[128,32,128]{2,1,0:T(8,128)} custom-call(f32[128,32,128]{2,1,0:T(8,128)} %get-tuple-element.7.packed_in, f32[64,128]{1,0:T(8,128)} %get-tuple-element.8.top_ref, f32[64,128]{1,0:T(8,128)} %get-tuple-element.9.wind_top_ref, f32[64,128]{1,0:T(8,128)} %collective-permute-done.same_ref, ...), custom_call_target="tpu_custom_call", output_to_operand_aliasing={{}: (0, {})} | custom-call | flops 100000 | bytes 300000 | tf_op jit(solution)/shard_map/pallas_call | solution.py:398
  18.8 12.9 %all-to-all-start = ((f32[128,32,128]{2,1,0:T(8,128)}), f32[128,32,128]{2,1,0:T(8,128)S(1)}, u32[]{:S(2)}, u32[]{:S(2)}) async-start(f32[128,32,128]{2,1,0:T(8,128)} %shard_map.115), calls=%async_computation | async-start | bytes 4194304 | tf_op jit(solution)/shard_map/all_to_all | solution.py:417
  31.7 2.9 %shard_map.117 = f32[32,64]{1,0:T(8,128)} custom-call(f32[64,32,128]{2,1,0:T(8,128)} %haze_ref.1, f32[32,64]{1,0:T(8,128)} %bitcast.10, f32[1,128]{1,0:T(1,128)} %bitcast.17), custom_call_target="tpu_custom_call" | custom-call | flops 400000000 | bytes 1000000 | tf_op jit(solution)/shard_map/pallas_call | solution.py:429
  34.6 49.7 %all-to-all-done.arrived_ref = f32[128,32,128]{2,1,0:T(8,128)S(1)} async-done(((f32[128,32,128]{2,1,0:T(8,128)}), f32[128,32,128]{2,1,0:T(8,128)S(1)}, u32[]{:S(2)}, u32[]{:S(2)}) %all-to-all-start) | async-done | bytes 2097184 | tf_op jit(solution)/shard_map/all_to_all | solution.py:417
  84.3 1.3 %shard_map.116 = f32[128,32,128]{2,1,0:T(8,128)} custom-call(f32[128,32,128]{2,1,0:T(8,128)S(1)} %all-to-all-done.arrived_ref), custom_call_target="tpu_custom_call" | custom-call | bytes 4000000 | tf_op jit(solution)/shard_map/pallas_call | solution.py:420
Async XLA Ops:
  2.6 6.8 %collective-permute-start = (f32[64,128]{1,0:T(8,128)}, f32[64,128]{1,0:T(8,128)}, u32[]{:S(2)}, u32[]{:S(2)}) collective-permute-start(f32[64,128]{1,0:T(8,128)} %shard_map.114), channel_id=1, source_target_pairs={{0,1},{1,2},{2,3},{3,4},{4,5},{5,6},{6,7},{7,0},{8,9},{9,10},{10,1... | collective-permute-start | bytes 98312 | tf_op jit(solution)/shard_map/ppermute | solution.py:372
  2.6 14.5 %collective-permute-start.1 = (f32[64,128]{1,0:T(8,128)}, f32[64,128]{1,0:T(8,128)}, u32[]{:S(2)}, u32[]{:S(2)}) collective-permute-start(f32[64,128]{1,0:T(8,128)} %shard_map.114), channel_id=1, source_target_pairs={{7,8},{15,16},{23,24},{31,32},{39,40},{47,48},{55,56},{63,64},{71,... | collective-permute-start | bytes 98312 | tf_op jit(solution)/shard_map/ppermute | solution.py:372
  3.9 13.2 %collective-permute-start.2 = (f32[64,128]{1,0:T(8,128)}, f32[64,128]{1,0:T(8,128)}, u32[]{:S(2)}, u32[]{:S(2)}) collective-permute-start(f32[64,128]{1,0:T(8,128)} %shard_map.114), channel_id=1, source_target_pairs={{7,504},{15,0},{23,8},{31,16},{39,24},{47,32},{55,40},{63,48},{71,... | collective-permute-start | bytes 98312 | tf_op jit(solution)/shard_map/ppermute | solution.py:372
  18.8 65.5 %all-to-all-start = ((f32[128,32,128]{2,1,0:T(8,128)}), f32[128,32,128]{2,1,0:T(8,128)S(1)}, u32[]{:S(2)}, u32[]{:S(2)}) async-start(f32[128,32,128]{2,1,0:T(8,128)} %shard_map.115), calls=%async_computation | async-start | bytes 4194304 | tf_op jit(solution)/shard_map/all_to_all | solution.py:417

commit v6 on v5

--- a/solution.py
+++ b/solution.py
@@ -255,8 +255,8 @@
     top_ref,
     wind_top_ref,
     same_ref,
+    high_ref,
     low_ref,
-    high_ref,
     slot_ref,
     source_ref,
     packed_hbm,
@@ -371,7 +371,7 @@
             route = [(flat(w, last), flat(w + distance, 0)) for w in range(wide_count)]
         return lax.ppermute(rim, both, route)
 
-    same, low, high = passed(0), passed(1), passed(-1)
+    same, high, low = passed(0), passed(-1), passed(1)
     packed_type = shape(slots, cells, bins)
     upwind_rows = upwind_blocks.reshape(-1, 128)
     packed, top, wind_top, slot, source = pl.pallas_call(
@@ -407,7 +407,7 @@
         ],
         input_output_aliases={0: 0},
         cost_estimate=cost(100000, 300000),
-    )(packed, top, wind_top, same, low, high, slot, source)
+    )(packed, top, wind_top, same, high, low, slot, source)
     lines = wide_count // COLUMNS
     order = [line * COLUMNS + column for column in range(COLUMNS) for line in range(lines)]
     groups = [

time: 86.1 us -> 84 us (0.976)
  the two profiles are of different devices: /device:TPU:24 before, /device:TPU:34 now
where the time goes in v6:
time: 84 us; the launch traced here: 83.5 us
  waiting for transfers between devices  52 us (62%)
  starting transfers between devices  18.8 us (22%)
  Pallas kernels  12 us (14%)
    all_to_all x1, waiting for transfers between devices, local(): lax.all_to_all(packed, both, split_axis=0, concat_axis=0, tiled=True, axi...  52 us
    all_to_all x1, starting transfers between devices, local(): lax.all_to_all(packed, both, split_axis=0, concat_axis=0, tiled=True, axi...  16.3 us
    pallas_call x1, Pallas kernels, local(): pl.pallas_call(pack_kernel, out_shape=(packed_type, rows_type, rows_type,...  4.2 us
    pallas_call x1, Pallas kernels, local(): pl.pallas_call(vapour_kernel, out_shape=shape(cells, blocks), in_specs=[w...  2.86 us
    ppermute x3, starting transfers between devices, passed(): return lax.ppermute(rim, both, route)  2.53 us
    pallas_call x1, Pallas kernels, local(): pl.pallas_call(rim_kernel, out_shape=rows_type, in_specs=[whole(pl.ANY)]...  1.95 us
  transfers between devices with their start and end apart: 4, of which 1 were waited for; matrix products, arithmetic and copies ran while one was open for 0% of the time, Pallas kernels for 8%

profile of v6, /device:TPU:34, one launch (start us, length us, event | category | flops | bytes accessed | tf_op | source)
XLA Modules:
  0.0 83.5 jit_solution(4813532430739128193)
XLA Ops:
  0.6 1.9 %shard_map.114 = f32[64,128]{1,0:T(8,128)} custom-call(f32[64,32,128]{2,1,0:T(8,128)} %haze_ref.1, f32[32,64]{1,0:T(8,128)} %bitcast.8, f32[1,128]{1,0:T(1,128)} %bitcast.15, f32[8,128]{1,0:T(8,128)} %bitcast.11, f32[8,128]{1,0:T(8,128)} %bitcast.13, f32[8,128]{1,0:T(8,128)} %gain_hbm.3, f32[8,128]{1,0:T(8,128)} %loss_hbm.3), custom_call_target="tpu_custom_call" | custom-call | flops 10000000 | bytes 100000 | tf_op jit(solution)/shard_map/pallas_call | solution.py:344
  2.6 0.0 collective-permute-start
  2.6 1.3 %collective-permute-start.1 = (f32[64,128]{1,0:T(8,128)}, f32[64,128]{1,0:T(8,128)}, u32[]{:S(2)}, u32[]{:S(2)}) collective-permute-start(f32[64,128]{1,0:T(8,128)} %shard_map.114), channel_id=1, source_target_pairs={{7,504},{15,0},{23,8},{31,16},{39,24},{47,32},{55,40},{63,48},{71,... | collective-permute-start | bytes 98312 | tf_op jit(solution)/shard_map/ppermute | solution.py:372
  3.9 1.2 %collective-permute-start.2 = (f32[64,128]{1,0:T(8,128)}, f32[64,128]{1,0:T(8,128)}, u32[]{:S(2)}, u32[]{:S(2)}) collective-permute-start(f32[64,128]{1,0:T(8,128)} %shard_map.114), channel_id=1, source_target_pairs={{7,8},{15,16},{23,24},{31,32},{39,40},{47,48},{55,56},{63,64},{71,... | collective-permute-start | bytes 98312 | tf_op jit(solution)/shard_map/ppermute | solution.py:372
  5.1 4.2 %shard_map.113 = (f32[128,32,128]{2,1,0:T(8,128)}, f32[64,128]{1,0:T(8,128)}, f32[64,128]{1,0:T(8,128)}, s32[64]{0:T(128)}, s32[1,128]{1,0:T(1,128)}) custom-call(f32[64,32,128]{2,1,0:T(8,128)} %haze_ref.1, f32[32,64]{1,0:T(8,128)} %bitcast.18, f32[32,64]{1,0:T(8,128)} %bitcast.9, f32[1,128]{1,0:T(1,128)} %bitcast.16, f32[8,128]{1,0:T(8,128)} %bitcast.12, ...), custom_call_target="tpu_custom_call" | custom-call | flops 800000000 | bytes 4000000 | tf_op jit(solution)/shard_map/pallas_call | solution.py:377
  9.3 0.0 collective-permute-done.same_ref
  9.3 0.0 collective-permute-done.1.high_ref
  9.4 0.0 collective-permute-done.2.low_ref
  9.4 1.7 %shard_map.115 = f32[128,32,128]{2,1,0:T(8,128)} custom-call(f32[128,32,128]{2,1,0:T(8,128)} %get-tuple-element.7.packed_in, f32[64,128]{1,0:T(8,128)} %get-tuple-element.8.top_ref, f32[64,128]{1,0:T(8,128)} %get-tuple-element.9.wind_top_ref, f32[64,128]{1,0:T(8,128)} %collective-permute-done.same_ref, ...), custom_call_target="tpu_custom_call", output_to_operand_aliasing={{}: (0, {})} | custom-call | flops 100000 | bytes 300000 | tf_op jit(solution)/shard_map/pallas_call | solution.py:398
  11.0 16.3 %all-to-all-start = ((f32[128,32,128]{2,1,0:T(8,128)}), f32[128,32,128]{2,1,0:T(8,128)S(1)}, u32[]{:S(2)}, u32[]{:S(2)}) async-start(f32[128,32,128]{2,1,0:T(8,128)} %shard_map.115), calls=%async_computation | async-start | bytes 4194304 | tf_op jit(solution)/shard_map/all_to_all | solution.py:417
  27.3 2.9 %shard_map.117 = f32[32,64]{1,0:T(8,128)} custom-call(f32[64,32,128]{2,1,0:T(8,128)} %haze_ref.1, f32[32,64]{1,0:T(8,128)} %bitcast.10, f32[1,128]{1,0:T(1,128)} %bitcast.17), custom_call_target="tpu_custom_call" | custom-call | flops 400000000 | bytes 1000000 | tf_op jit(solution)/shard_map/pallas_call | solution.py:429
  30.2 52.0 %all-to-all-done.arrived_ref = f32[128,32,128]{2,1,0:T(8,128)S(1)} async-done(((f32[128,32,128]{2,1,0:T(8,128)}), f32[128,32,128]{2,1,0:T(8,128)S(1)}, u32[]{:S(2)}, u32[]{:S(2)}) %all-to-all-start) | async-done | bytes 2097184 | tf_op jit(solution)/shard_map/all_to_all | solution.py:417
  82.2 1.3 %shard_map.116 = f32[128,32,128]{2,1,0:T(8,128)} custom-call(f32[128,32,128]{2,1,0:T(8,128)S(1)} %all-to-all-done.arrived_ref), custom_call_target="tpu_custom_call" | custom-call | bytes 4000000 | tf_op jit(solution)/shard_map/pallas_call | solution.py:420
Async XLA Ops:
  2.6 6.7 %collective-permute-start = (f32[64,128]{1,0:T(8,128)}, f32[64,128]{1,0:T(8,128)}, u32[]{:S(2)}, u32[]{:S(2)}) collective-permute-start(f32[64,128]{1,0:T(8,128)} %shard_map.114), channel_id=1, source_target_pairs={{0,1},{1,2},{2,3},{3,4},{4,5},{5,6},{6,7},{7,0},{8,9},{9,10},{10,1... | collective-permute-start | bytes 98312 | tf_op jit(solution)/shard_map/ppermute | solution.py:372
  2.6 6.7 %collective-permute-start.1 = (f32[64,128]{1,0:T(8,128)}, f32[64,128]{1,0:T(8,128)}, u32[]{:S(2)}, u32[]{:S(2)}) collective-permute-start(f32[64,128]{1,0:T(8,128)} %shard_map.114), channel_id=1, source_target_pairs={{7,504},{15,0},{23,8},{31,16},{39,24},{47,32},{55,40},{63,48},{71,... | collective-permute-start | bytes 98312 | tf_op jit(solution)/shard_map/ppermute | solution.py:372
  3.9 5.5 %collective-permute-start.2 = (f32[64,128]{1,0:T(8,128)}, f32[64,128]{1,0:T(8,128)}, u32[]{:S(2)}, u32[]{:S(2)}) collective-permute-start(f32[64,128]{1,0:T(8,128)} %shard_map.114), channel_id=1, source_target_pairs={{7,8},{15,16},{23,24},{31,32},{39,40},{47,48},{55,56},{63,64},{71,... | collective-permute-start | bytes 98312 | tf_op jit(solution)/shard_map/ppermute | solution.py:372
  11.0 71.2 %all-to-all-start = ((f32[128,32,128]{2,1,0:T(8,128)}), f32[128,32,128]{2,1,0:T(8,128)S(1)}, u32[]{:S(2)}, u32[]{:S(2)}) async-start(f32[128,32,128]{2,1,0:T(8,128)} %shard_map.115), calls=%async_computation | async-start | bytes 4194304 | tf_op jit(solution)/shard_map/all_to_all | solution.py:417
